TPU v7x, 128 devices: a whole 4x4x4 slice. The times are simulated.
128 devices in a mesh: mid: 8 (over x, y_hi), off: 16 (over z, y_lo, core).
Axes of the slice: x: 4, y: 4 (y_hi: 2, y_lo: 2; y = y_hi * 2 + y_lo), z: 4, core: 2. Of those that a mesh axis runs over, the one named last changes fastest.
Arguments:
- bins_data: bfloat16 [16, 64, 2, 2048], P('off', None, None, 'mid'), may hold values from -6 to 6
- operators: bfloat16 [16, 16, 128, 128], P('off'), may hold values from -0.5 to 0.5
- targets: int32 [16, 16], P('off'), may hold values from 0 to 255
- counts: int32 [16], P('off'), may hold values from 1 to 16, 128 in all
- layer_index: int32 [2, 8, 16], P(None, None, 'mid'), may hold values from 0 to 15
- slowness: float32 [2, 16], replicated, may hold values from 0.8 to 1.25
Outputs:
- wavefield: float32 [64, 256, 2, 2048], P('off', None, None, 'mid')
Inputs may be any that keep to these rules, and one draw needn't show every extreme that they name: Slots at positions counts[b] and beyond of bin b's list are unused; some bin has all 16 slots live.
All inputs are finite; a program needn't handle non-finite values. No bound on the sum of `counts` on one device may be relied on, other than what follows from the above.
Results may differ from a plain program's by a relative error of at most 0.0003.
Values may be sent and summed in bfloat16 or wider, within the bound.
A program may use at most 128 MiB of HBM per device.

v0:
```python
import math

import jax
import jax.numpy as jnp
from jax import lax
from jax.sharding import PartitionSpec as P

NH = 256
BLK = 128


dz_cells = 2.0
damping = 0.1


def signed_wave(index, length):
    signed = (index + length // 2) % length - length // 2
    return signed.astype(jnp.float32) * (2.0 * math.pi / length)


def root_pair(level):
    magnitude = jnp.sqrt(level * level + damping * damping)
    larger = jnp.sqrt(0.5 * (magnitude + jnp.abs(level)))
    smaller = damping / (2.0 * larger)
    return (jnp.where(level >= 0, larger, smaller), jnp.where(level >= 0, smaller, larger))


def propagator(omega_sq, mid_wave, offset_wave):
    source = 0.5 * (mid_wave - offset_wave)
    receiver = 0.5 * (mid_wave + offset_wave)
    real_s, imag_s = root_pair(omega_sq - source * source)
    real_r, imag_r = root_pair(omega_sq - receiver * receiver)
    decay = jnp.exp(-dz_cells * (imag_s + imag_r))
    turn = dz_cells * (real_s + real_r)
    return (decay * jnp.cos(turn), decay * jnp.sin(turn))


def angle_table(rows_n, cols_n, modulus):
    left = lax.broadcasted_iota(jnp.int32, (rows_n, cols_n), 0)
    right = lax.broadcasted_iota(jnp.int32, (rows_n, cols_n), 1)
    angles = (left * right % modulus).astype(jnp.float32) * (2.0 * math.pi / modulus)
    return (jnp.cos(angles), jnp.sin(angles))


def multiply(real_a, imag_a, real_b, imag_b):
    return (real_a * real_b - imag_a * imag_b, real_a * imag_b + imag_a * real_b)


def contract(form, left, right):
    return jnp.einsum(
        form, left, right, precision=lax.Precision.HIGHEST, preferred_element_type=jnp.float32
    )


def apply_block(source, weight_block):
    return jnp.dot(
        source.reshape(-1, weight_block.shape[0]), weight_block, preferred_element_type=jnp.float32
    ).reshape(source.shape)


def offset_forward(form, real_in, imag_in, cos_h, sin_h):
    real_out = contract(form, real_in, cos_h) + contract(form, imag_in, sin_h)
    imag_out = contract(form, imag_in, cos_h) - contract(form, real_in, sin_h)
    return jnp.stack([real_out, imag_out], 2)


def offset_inverse(spectrum, cos_h, sin_h):
    real_in = spectrum[:, :, 0]
    imag_in = spectrum[:, :, 1]
    scale = 1.0 / cos_h.shape[0]
    real_out = (
        contract("fkm,kh->fhm", real_in, cos_h) - contract("fkm,kh->fhm", imag_in, sin_h)
    ) * scale
    imag_out = (
        contract("fkm,kh->fhm", imag_in, cos_h) + contract("fkm,kh->fhm", real_in, sin_h)
    ) * scale
    return (real_out, imag_out)


def midpoint_step(spectrum, omega_sq, offset_wave):
    frames = spectrum.shape[0]
    rows_here = spectrum.shape[1]
    total_mid = spectrum.shape[3]
    outer = total_mid // 128
    cos_a, sin_a = angle_table(outer, outer, outer)
    cos_t, sin_t = angle_table(outer, 128, total_mid)
    cos_b, sin_b = angle_table(128, 128, 128)
    real_in = spectrum[:, :, 0].reshape(frames, rows_here, outer, 128)
    imag_in = spectrum[:, :, 1].reshape(frames, rows_here, outer, 128)
    real_one = contract("fhab,ak->fhkb", real_in, cos_a) + contract("fhab,ak->fhkb", imag_in, sin_a)
    imag_one = contract("fhab,ak->fhkb", imag_in, cos_a) - contract("fhab,ak->fhkb", real_in, sin_a)
    real_two, imag_two = multiply(real_one, imag_one, cos_t, -sin_t)
    real_three = contract("fhkb,bl->fhkl", real_two, cos_b) + contract(
        "fhkb,bl->fhkl", imag_two, sin_b
    )
    imag_three = contract("fhkb,bl->fhkl", imag_two, cos_b) - contract(
        "fhkb,bl->fhkl", real_two, sin_b
    )
    wave_index = lax.broadcasted_iota(jnp.int32, (outer, 128), 0) + outer * lax.broadcasted_iota(
        jnp.int32, (outer, 128), 1
    )
    mid_wave = signed_wave(wave_index, total_mid)
    phase_real, phase_imag = propagator(
        omega_sq[:, None, None, None], mid_wave[None, None], offset_wave[None, :, None, None]
    )
    real_four, imag_four = multiply(real_three, imag_three, phase_real, phase_imag)
    real_five = contract("fhkl,lb->fhkb", real_four, cos_b) - contract(
        "fhkl,lb->fhkb", imag_four, sin_b
    )
    imag_five = contract("fhkl,lb->fhkb", imag_four, cos_b) + contract(
        "fhkl,lb->fhkb", real_four, sin_b
    )
    real_six, imag_six = multiply(real_five, imag_five, cos_t, sin_t)
    real_out = contract("fhkb,ka->fhab", real_six, cos_a) - contract(
        "fhkb,ka->fhab", imag_six, sin_a
    )
    imag_out = contract("fhkb,ka->fhab", imag_six, cos_a) + contract(
        "fhkb,ka->fhab", real_six, sin_a
    )
    scale = 1.0 / total_mid
    return jnp.stack(
        [
            real_out.reshape(frames, rows_here, total_mid) * scale,
            imag_out.reshape(frames, rows_here, total_mid) * scale,
        ],
        2,
    )


def split_step(real_in, imag_in, omega_values, layer_rows, slow_row):
    layer_total = slow_row.shape[0]
    picks = (
        layer_rows[:, :, None] == lax.broadcasted_iota(jnp.int32, (1, 1, layer_total), 2)
    ).astype(jnp.float32)
    block_slow = jnp.sum(picks * slow_row[None, None, :], axis=2)
    heights, widths = block_slow.shape
    cell_slow = jnp.broadcast_to(
        block_slow[:, None, :, None], (heights, NH // heights, widths, BLK)
    ).reshape(NH, widths * BLK)
    turn = 2.0 * dz_cells * omega_values[:, None, None] * (cell_slow - 1.0)[None]
    real_out, imag_out = multiply(real_in, imag_in, jnp.cos(turn), jnp.sin(turn))
    return jnp.stack([real_out, imag_out], 2)


def local(bins_data, operators, targets, counts, layer_index, slowness):
    off_count = lax.axis_size("off")
    mid_count = lax.axis_size("mid")
    freq_total = bins_data.shape[1]
    freq_local = freq_total // off_count
    mid_local = bins_data.shape[3]
    first_form = "fhm,hk->fkm"
    partial_term = jnp.zeros(
        (NH // off_count * lax.axis_size("off"), freq_total, 2, mid_local), jnp.float32
    )
    source = bins_data[0]
    weights_here = operators[0]
    targets_here = targets[0]

    def add_slot(entry_at, current):
        weight_block = lax.dynamic_index_in_dim(weights_here, entry_at, 0, False)
        target_row = lax.dynamic_index_in_dim(targets_here, entry_at, 0, False)
        inside = ((target_row >= 0) & (target_row < NH // off_count * lax.axis_size("off"))).astype(
            jnp.float32
        )
        placed = jnp.clip(target_row, 0, NH // off_count * lax.axis_size("off") - 1)
        added = apply_block(source, weight_block) * inside
        before = lax.dynamic_index_in_dim(current, placed, 0, True)
        return lax.dynamic_update_index_in_dim(current, before + added[None], placed, 0)

    partial_term = lax.fori_loop(0, counts[0], add_slot, partial_term)
    owned = lax.psum_scatter(partial_term, "off", scatter_dimension=0, tiled=True)
    by_freq = lax.all_to_all(owned, "off", split_axis=1, concat_axis=0, tiled=True)
    first_form = "hfm,hk->fkm"
    real_in = by_freq[:, :, 0]
    imag_in = by_freq[:, :, 1]
    cos_h, sin_h = angle_table(NH, NH, NH)
    freq_index = lax.axis_index("off") * freq_local + lax.broadcasted_iota(
        jnp.int32, (freq_local,), 0
    )
    omega_values = math.pi * (0.1 + 0.8 * (freq_index.astype(jnp.float32) + 0.5) / freq_total)
    omega_sq = omega_values * omega_values
    rows_mid = NH // mid_count
    offset_index = lax.axis_index("mid") * rows_mid + lax.broadcasted_iota(
        jnp.int32, (rows_mid,), 0
    )
    offset_wave = signed_wave(offset_index, NH)
    current_form = first_form
    for depth_step in range(layer_index.shape[0]):
        spectrum = offset_forward(current_form, real_in, imag_in, cos_h, sin_h)
        across = lax.all_to_all(spectrum, "mid", split_axis=1, concat_axis=3, tiled=True)
        across = midpoint_step(across, omega_sq, offset_wave)
        returned = lax.all_to_all(across, "mid", split_axis=3, concat_axis=1, tiled=True)
        real_h, imag_h = offset_inverse(returned, cos_h, sin_h)
        wavefield = split_step(
            real_h, imag_h, omega_values, layer_index[depth_step], slowness[depth_step]
        )
        real_in = wavefield[:, :, 0]
        imag_in = wavefield[:, :, 1]
        current_form = "fhm,hk->fkm"
    return wavefield


def solution(mesh):
    in_specs = (
        P("off", None, None, "mid"),
        P("off", None, None, None),
        P("off", None),
        P("off"),
        P(None, None, "mid"),
        P(),
    )
    out_specs = P("off", None, None, "mid")
    return jax.shard_map(local, mesh=mesh, in_specs=in_specs, out_specs=out_specs, check_vma=False)
```

profile of v0, /device:TPU:1, one launch (start us, length us, event | category | flops | bytes accessed | tf_op | source)
XLA Modules:
  0.0 895.7 jit_solution(2872606088279803071)
XLA Ops:
  7.4 11.3 %broadcast_in_dim.7.clone = f32[256,64,2,256]{3,1,2,0:T(8,128)} broadcast(f32[]{:T(128)} %constant.156.clone.1), dimensions={} | broadcast | bytes 33554436 | tf_op jit(solution)/shard_map/broadcast_in_dim | solution.py:152
  18.7 55.4 %while.11 = (s32[]{:T(128)}, f32[256,64,2,256]{3,1,2,0:T(8,128)}, s32[]{:T(128)}, s32[16]{0:T(128)S(1)}, bf16[16,128,128]{2,1,0:T(8,128)(2,1)}, /*index=5*/bf16[...) while((s32[]{:T(128)}, f32[256,64,2,256]{3,1,2,0:T(8,128)}, ...), condition=%wide.wide.region_1.2_spmd, body=%wide.wide.region_0.1_spmd.sunk | while | flops 8454155 | bytes 1672421 | solution.py:170
  74.2 395.1 %reduce-scatter.2.cloned.1.call-done = f32[16,64,2,256]{3,1,2,0:T(8,128)} async-done(((f32[256,64,2,256]{3,1,2,0:T(8,128)}), f32[16,64,2,256]{3,1,2,0:T(8,128)}) %reduce-scatter.2.cloned.1.call-update) | async-done | bytes 2097168 | tf_op jit(solution)/shard_map/reduce_scatter | solution.py:171
  469.3 3.2 copy.60
  472.5 31.7 %all_to_all.90 = f32[16,64,2,256]{3,2,0,1:T(2,128)S(1)} all-to-all(f32[16,64,2,256]{3,2,0,1:T(2,128)S(1)} %copy.60), channel_id=1, replica_groups=mesh['mid'=8,'off'=16] {'off'}, dimensions={1} | all-to-all | bytes 4194304 | tf_op jit(solution)/shard_map/all_to_all | solution.py:172
  504.4 2.0 fusion.81
  506.5 2.0 fusion.82
  508.5 2.1 fusion.31
  510.6 2.0 fusion.30
  512.8 2.7 copy.62
  515.4 6.2 all-to-all-start.1
  522.7 28.8 %all-to-all-done.1 = f32[4,256,2,256]{3,0,2,1:T(4,128)S(1)} async-done(((f32[4,256,2,256]{3,0,2,1:T(4,128)}), f32[4,256,2,256]{3,0,2,1:T(4,128)S(1)}, u32[]{:S(2)}, u32[]{:S(2)}) %all-to-all-start.1) | async-done | bytes 2097184 | tf_op jit(solution)/shard_map/all_to_all | solution.py:190
  551.5 2.5 copy.101
  554.0 1.9 all_to_all.72
  563.2 1.2 convolution_add_fusion.6
  565.7 7.6 fusion.152
  573.3 7.3 fusion.150
  580.7 7.2 convolution_subtract_fusion.5
  587.9 7.4 convolution_add_fusion.5
  597.4 2.0 fusion.19
  599.4 3.6 copy.79
  603.0 2.0 fusion.17
  605.1 3.6 copy.80
  608.7 7.7 fusion.433
  616.4 9.5 %reshape.232 = f32[8,1,65536]{2,1,0:T(1,128)} reshape(f32[2048,2,4,32]{3,2,1,0:T(4,128)} %fusion.433) | data formatting | bytes 4194304
  625.9 4.1 all-to-all-start.2
  630.5 28.9 %all-to-all-done.2 = f32[8,1,65536]{2,1,0:T(1,128)S(1)} async-done(((f32[8,1,65536]{2,1,0:T(1,128)}), f32[8,1,65536]{2,1,0:T(1,128)S(1)}, u32[]{:S(2)}, u32[]{:S(2)}) %all-to-all-start.2) | async-done | bytes 2097184 | tf_op jit(solution)/shard_map/all_to_all | solution.py:192
  659.4 1.3 copy-done
  661.3 7.3 reduce
  668.6 7.6 reshape.233
  676.2 6.8 copy.66
  683.0 2.0 fusion.84
  685.1 2.0 fusion.83
  687.1 2.1 fusion.27
  689.1 2.1 fusion.29
  691.2 6.0 fusion.106
  697.2 5.8 fusion.104
  703.1 6.2 fusion.25
  709.3 5.8 fusion.24
  715.4 1.4 copy.68
  716.8 27.9 %all_to_all.91 = f32[4,256,2,256]{3,0,2,1:T(4,128)S(1)} all-to-all(f32[4,256,2,256]{3,0,2,1:T(4,128)S(1)} %copy.68), channel_id=1, replica_groups=mesh['mid'=8,'off'=16] {'mid'}, dimensions={1} | all-to-all | bytes 4194304 | tf_op jit(solution)/shard_map/all_to_all | solution.py:190
  744.7 2.5 copy.100
  747.2 1.9 all_to_all.80
  756.4 1.2 convolution_add_fusion.2
  758.9 7.4 fusion.146
  766.3 7.6 fusion.144
  773.9 7.2 convolution_subtract_fusion.1
  781.1 7.3 convolution_add_fusion.1
  790.5 2.0 fusion.15
  792.6 3.6 copy.81
  796.2 2.0 fusion.13
  798.2 3.6 copy.82
  801.8 7.7 fusion.432
  809.6 9.5 %reshape.234 = f32[8,1,65536]{2,1,0:T(1,128)} reshape(f32[2048,2,4,32]{3,2,1,0:T(4,128)} %fusion.432) | data formatting | bytes 4194304
  819.0 4.6 all-to-all-start.4
  823.9 27.7 %all-to-all-done.4 = f32[8,1,65536]{2,1,0:T(1,128)} async-done(((f32[8,1,65536]{2,1,0:T(1,128)}), f32[8,1,65536]{2,1,0:T(1,128)}, u32[]{:S(2)}, u32[]{:S(2)}) %all-to-all-start.4) | async-done | bytes 2097184 | tf_op jit(solution)/shard_map/all_to_all | solution.py:192
  851.6 7.3 reduce.1
  858.8 7.6 reshape.235
  866.4 6.9 copy.72
  873.4 2.0 fusion.86
  875.4 2.0 fusion.85
  877.4 2.1 fusion.21
  879.5 5.8 fusion.42
  885.5 2.9 copy.74
  (124 shorter events, 56.4 us)
Async XLA Ops:
  6.5 462.7 %reduce-scatter.2.cloned.1.call-start = ((), (), s32[]{:S(2)}) async-start(), calls=%async_computation.6 | async-start | bytes 35651584 | tf_op jit(solution)/shard_map/reduce_scatter | solution.py:171
  7.4 11.3 %copy-start.5 = (s32[1,16]{1,0:T(1,128)S(1)}, s32[1,16]{1,0:T(1,128)}, u32[]{:S(2)}) copy-start(s32[1,16]{1,0:T(1,128)} %param.10) | copy-start | bytes 196
  515.4 36.0 %all-to-all-start.1 = ((f32[4,256,2,256]{3,0,2,1:T(4,128)}), f32[4,256,2,256]{3,0,2,1:T(4,128)S(1)}, u32[]{:S(2)}, u32[]{:S(2)}) async-start(f32[4,256,2,256]{3,0,2,1:T(4,128)} %copy.62), calls=%async_computation.2 | async-start | bytes 4194304 | tf_op jit(solution)/shard_map/all_to_all | solution.py:190
  564.5 1.2 copy-start.1
  625.9 4.2 copy-start.4
  625.9 4.2 copy-start.3
  625.9 33.5 %all-to-all-start.2 = ((f32[8,1,65536]{2,1,0:T(1,128)}), f32[8,1,65536]{2,1,0:T(1,128)S(1)}, u32[]{:S(2)}, u32[]{:S(2)}) async-start(f32[8,1,65536]{2,1,0:T(1,128)} %reshape.232), calls=%async_computation.3 | async-start | bytes 4194304 | tf_op jit(solution)/shard_map/all_to_all | solution.py:192
  659.4 1.3 copy-start
  757.6 1.2 copy-start.2
  819.0 32.5 %all-to-all-start.4 = ((f32[8,1,65536]{2,1,0:T(1,128)}), f32[8,1,65536]{2,1,0:T(1,128)}, u32[]{:S(2)}, u32[]{:S(2)}) async-start(f32[8,1,65536]{2,1,0:T(1,128)} %reshape.234), calls=%async_computation.5 | async-start | bytes 4194304 | tf_op jit(solution)/shard_map/all_to_all | solution.py:192
Sparse Core Ops, SparseCore 0:
  74.3 394.9 reduce-scatter.1
where the time goes:
time: 905 us; the launch traced here: 896 us
  waiting for transfers between devices  480 us (53%)
  matrix products  150 us (17%)
  local copies, waits for them, and re-layouts  119 us (13%)
  blocking collectives  59.6 us (7%)
  other arithmetic  32.9 us (4%)
  loops' own time  24.2 us (3%)
  starting transfers between devices  14.9 us (2%)
  between operations  14.5 us (2%)
    reduce_scatter x1, waiting for transfers between devices, local(): lax.psum_scatter(partial_term, 'off', scatter_dimension=0, tiled=True)  395 us
    dot_general x48, matrix products, contract(): jnp.einsum(form, left, right, precision=lax.Precision.HIGHEST, preferred_...  142 us
    all_to_all x2, waiting for transfers between devices, local(): lax.all_to_all(across, 'mid', split_axis=3, concat_axis=1, tiled=True)  56.6 us
    unnamed x22, local copies, waits for them, and re-layouts  36.3 us
    all_to_all x1, blocking collectives, local(): lax.all_to_all(owned, 'off', split_axis=1, concat_axis=0, tiled=True)  31.7 us
    all_to_all x1, waiting for transfers between devices, local(): lax.all_to_all(spectrum, 'mid', split_axis=1, concat_axis=3, tiled=True)  28.8 us
    all_to_all x1, blocking collectives, local(): lax.all_to_all(spectrum, 'mid', split_axis=1, concat_axis=3, tiled=True)  27.9 us
    another operation x1, loops' own time, local(): partial_term = lax.fori_loop(0, counts[0], add_slot, partial_term)  24.2 us
  transfers between devices with their start and end apart: 4, of which 4 were waited for; matrix products, arithmetic and copies ran while one was open for 0% of the time, Pallas kernels for 0%

commit v1 on v0

v1 whole, which is shorter than its diff:
```python
import functools
import math

import jax
import jax.numpy as jnp
import numpy as np
from jax import lax
from jax.experimental import pallas as pl
from jax.experimental.pallas import tpu as pltpu
from jax.sharding import PartitionSpec as P


NF = 64
NH = 256
NM = 2048
BLK = 128
ENT = 16
NB = 16
MID = 8
OFF = 16
DZ = 2.0
DAMP = 0.1
MESH = pl.DeviceIdType.MESH
VM = pl.BlockSpec(memory_space=pltpu.VMEM)
F32 = jnp.float32
BF16 = jnp.bfloat16


def halves(table):
    high = np.asarray(table, np.float32).astype(jnp.bfloat16)
    low = (np.asarray(table, np.float64) - high.astype(np.float64)).astype(np.float32)
    return high, low.astype(jnp.bfloat16)


def offset_tables():
    wave = np.array([(2 * (s - 64) + p) % NH for p in range(2) for s in range(128)])
    place = np.arange(NH)
    angle = 2.0 * np.pi * (np.outer(wave, place) % NH) / NH
    cos, sin = np.cos(angle).reshape(2, 128, NH), np.sin(angle).reshape(2, 128, NH)
    forward = np.zeros((2, 2, 128, 2, NH))
    forward[:, 0, :, 0], forward[:, 0, :, 1] = cos, sin
    forward[:, 1, :, 0], forward[:, 1, :, 1] = -sin, cos
    inverse = np.zeros((2, NH, 2, 2, 128))
    cos_t, sin_t = cos.transpose(2, 0, 1), sin.transpose(2, 0, 1)
    inverse[0, :, :, 0], inverse[0, :, :, 1] = cos_t, -sin_t
    inverse[1, :, :, 0], inverse[1, :, :, 1] = sin_t, cos_t
    return halves(forward.reshape(512, 512)), halves(inverse.reshape(512, 512) / NH)


def midpoint_tables():
    inner = np.arange(128)
    wave = (np.arange(128) + 64) % 128
    angle = 2.0 * np.pi * (np.outer(inner, wave) % 128) / 128
    cos, sin = np.cos(angle), np.sin(angle)
    forward = np.block([[cos, -sin], [sin, cos]])
    inverse = np.block([[cos.T, sin.T], [-sin.T, cos.T]]) / NM
    turn = 2.0 * np.pi * np.outer(np.arange(16), inner) / NM
    twiddle = np.stack([np.cos(turn), np.sin(turn)], 1)
    twiddle = np.broadcast_to(twiddle[:, :, None], (16, 2, 8, 128)).astype(np.float32)
    return halves(forward), halves(inverse), np.ascontiguousarray(twiddle)


def split(x):
    high = x.astype(BF16)
    return high, (x - high.astype(F32)).astype(BF16)


def dot(a, b):
    return jnp.dot(a, b, preferred_element_type=F32)


def dot_table_left(high, low, x):
    x_high, x_low = split(x)
    return dot(high, x_high) + (dot(high, x_low) + dot(low, x_high))


def dot_table_right(x, high, low):
    x_high, x_low = split(x)
    return dot(x_high, high) + (dot(x_low, high) + dot(x_high, low))


def times_root(value, step, sign):
    real, imag = value
    step = step % 16
    if step == 0:
        return value
    if step == 4:
        return (-imag * sign, real * sign)
    half = float(np.sqrt(0.5))
    if step == 2:
        return ((real - sign * imag) * half, (imag + sign * real) * half)
    if step == 6:
        return ((-real - sign * imag) * half, (-imag + sign * real) * half)
    c, s = math.cos(2 * math.pi * step / 16), sign * math.sin(2 * math.pi * step / 16)
    return (real * c - imag * s, real * s + imag * c)


def small_fft(values, sign):
    n = len(values)
    if n == 1:
        return values
    even, odd = small_fft(values[0::2], sign), small_fft(values[1::2], sign)
    odd = [times_root(v, k * (16 // n), sign) for k, v in enumerate(odd)]
    return [(e[0] + o[0], e[1] + o[1]) for e, o in zip(even, odd)] + [
        (e[0] - o[0], e[1] - o[1]) for e, o in zip(even, odd)
    ]


def place_here():
    return lax.axis_index("mid"), lax.axis_index("off")


def pair_barrier():
    j, o = place_here()
    partner = o + 1 - 2 * lax.rem(o, 2)
    barrier = pltpu.get_barrier_semaphore()
    pl.semaphore_signal(barrier, inc=1, device_id=(j, partner), device_id_type=MESH)
    pl.semaphore_wait(barrier, 1)
    return j, partner


def wait_bytes(ref, sem):
    pltpu.make_async_copy(ref, ref, sem).wait()


def scatter_kernel(
    s_ref, row_ref, slow_ref, r_ref, rows_ref, slows_ref, ssem, rsem, msem, nsem, tsem
):
    j, o = place_here()
    me = j * OFF + o
    total = MID * OFF
    barrier = pltpu.get_barrier_semaphore()

    def signal(i, _):
        peer = lax.rem(me + i, total)
        pl.semaphore_signal(
            barrier, inc=1, device_id=(peer // OFF, lax.rem(peer, OFF)), device_id_type=MESH
        )
        return 0

    lax.fori_loop(1, total, signal, 0)
    pl.semaphore_wait(barrier, total - 1)

    own_row = pltpu.make_async_copy(row_ref, rows_ref.at[o], msem)
    own_row.start()
    own_slow = pltpu.make_async_copy(slow_ref, slows_ref.at[j], nsem)
    own_slow.start()

    def send_row(i, _):
        peer = lax.rem(o + i, OFF)
        pltpu.make_async_remote_copy(
            row_ref, rows_ref.at[o], tsem.at[0], msem, device_id=(j, peer), device_id_type=MESH
        ).start()
        return 0

    lax.fori_loop(1, OFF, send_row, 0)

    def send_slow(i, _):
        peer = lax.rem(j + i, MID)
        pltpu.make_async_remote_copy(
            slow_ref, slows_ref.at[j], tsem.at[1], nsem, device_id=(peer, o), device_id_type=MESH
        ).start()
        return 0

    lax.fori_loop(1, MID, send_slow, 0)

    def send(i, _):
        peer_j, peer_o = lax.rem(j + i // OFF, MID), lax.rem(o + lax.rem(i, OFF), OFF)
        pltpu.make_async_remote_copy(
            s_ref.at[peer_j, peer_o],
            r_ref.at[j, :, o],
            ssem,
            rsem,
            device_id=(peer_j, peer_o),
            device_id_type=MESH,
        ).start()
        return 0

    lax.fori_loop(1, total, send, 0)
    pltpu.make_async_copy(s_ref.at[j, o], r_ref.at[j, :, o], rsem).start()

    wait_bytes(rows_ref, msem)
    wait_bytes(slows_ref, nsem)
    wait_bytes(rows_ref.at[pl.ds(0, OFF - 1)], tsem.at[0])
    wait_bytes(slows_ref.at[pl.ds(0, MID - 1)], tsem.at[1])
    wait_bytes(r_ref, rsem)
    wait_bytes(s_ref.at[0, pl.ds(0, OFF - 1)], ssem)
    wait_bytes(s_ref.at[pl.ds(1, MID - 1)], ssem)


def scatter(chunks, row, slow):
    return pl.pallas_call(
        scatter_kernel,
        out_shape=[
            jax.ShapeDtypeStruct((MID, 2, NB, ENT, 128), F32),
            jax.ShapeDtypeStruct((NB, 8, NH), jnp.int32),
            jax.ShapeDtypeStruct((MID, 2, 8, 128), F32),
        ],
        in_specs=[VM] * 3,
        out_specs=[VM] * 3,
        scratch_shapes=[pltpu.SemaphoreType.DMA] * 4 + [pltpu.SemaphoreType.DMA((2,))],
        compiler_params=pltpu.CompilerParams(
            collective_id=0, has_side_effects=True, vmem_limit_bytes=40 << 20
        ),
        name="scatter_slots",
    )(chunks, row, slow)


def send_piece(source, target, place, partner, ssem, rsem):
    j = lax.axis_index("mid")
    copy = pltpu.make_async_remote_copy(
        source, target, ssem, rsem.at[place], device_id=(j, partner), device_id_type=MESH
    )
    copy.start()
    return copy


def to_waves_kernel(high_ref, low_ref, rows_ref, r_ref, q_ref, w_high, w_low, away, ssem, rsem):
    core = lax.rem(lax.axis_index("off"), 2)
    j, partner = pair_barrier()
    row = jnp.sum(rows_ref[:, 0, :], axis=0, keepdims=True) - 1
    pick = (lax.broadcasted_iota(jnp.int32, (NH, NB * ENT), 0) == row).astype(F32).astype(BF16)
    for part in range(2):
        cols = pl.ds(part * NH, NH)
        w_high[:, cols] = dot(high_ref[:, cols], pick).astype(BF16)
        w_low[:, cols] = dot(low_ref[:, cols], pick).astype(BF16)
    copies = []
    for pair in range(MID // 2):
        both = jnp.concatenate(
            [
                jnp.concatenate(
                    [r_ref[2 * pair + q, part].reshape(NB * ENT, 128) for q in range(2)], axis=1
                )
                for part in range(2)
            ],
            axis=0,
        )
        out = dot_table_left(w_high[...], w_low[...], both)
        copies += store_waves(out, pair, core, partner, q_ref, away, ssem, rsem)
    for copy in copies:
        copy.wait()


def store_waves(out, pair, core, partner, q_ref, away, ssem, rsem):
    copies = []
    for q in range(2):
        for part in range(2):
            even = out[part * 128 : (part + 1) * 128, q * 128 : (q + 1) * 128]
            odd = out[256 + part * 128 : 256 + (part + 1) * 128, q * 128 : (q + 1) * 128]
            q_ref[core, part, 2 * pair + q] = jnp.where(core == 0, even, odd)
            away[part, 2 * pair + q] = jnp.where(core == 0, odd, even)
    where = (slice(None), pl.ds(2 * pair, 2))
    copies.append(
        send_piece(
            away.at[where],
            q_ref.at[(core,) + where],
            pair,
            partner,
            ssem.at[pair],
            rsem,
        )
    )
    return copies


def exchange_call(kernel, name, out, extra, cid, *args):
    return pl.pallas_call(
        kernel,
        out_shape=jax.ShapeDtypeStruct(out, F32),
        in_specs=[VM] * len(args),
        out_specs=VM,
        scratch_shapes=extra + [pltpu.SemaphoreType.DMA((4,))] * 2,
        compiler_params=pltpu.CompilerParams(
            collective_id=cid, has_side_effects=True, vmem_limit_bytes=56 << 20
        ),
        name=name,
    )(*args)


FIELD = (2, 2, MID, 128, 128)


def midpoint_chunk(q_ref, out_ref, phase_ref, tw_ref, fwd, inv, work, at):
    for sub in range(4):
        rows = pl.ds(at + sub * 8, 8)
        values = [
            (q_ref[a % 2, 0, a // 2, rows, :], q_ref[a % 2, 1, a // 2, rows, :]) for a in range(16)
        ]
        values = small_fft(values, -1)
        for k, (real, imag) in enumerate(values):
            cos, sin = tw_ref[k, 0], tw_ref[k, 1]
            here = pl.ds(k * 32 + sub * 8, 8)
            work[here, 0:128] = real * cos + imag * sin
            work[here, 128:256] = imag * cos - real * sin
    for k in range(16):
        here = pl.ds(k * 32, 32)
        z = dot_table_right(work[here, :], fwd[0][...], fwd[1][...])
        real, imag = z[:, :128], z[:, 128:]
        turn_r = phase_ref[0, k, pl.ds(at, 32), :]
        turn_i = phase_ref[1, k, pl.ds(at, 32), :]
        z = jnp.concatenate(
            [real * turn_r - imag * turn_i, real * turn_i + imag * turn_r], axis=1
        )
        work[here, :] = dot_table_right(z, inv[0][...], inv[1][...])
    for sub in range(4):
        rows = pl.ds(at + sub * 8, 8)
        values = []
        for k in range(16):
            here = pl.ds(k * 32 + sub * 8, 8)
            real, imag = work[here, 0:128], work[here, 128:256]
            cos, sin = tw_ref[k, 0], tw_ref[k, 1]
            values.append((real * cos - imag * sin, real * sin + imag * cos))
        values = small_fft(values, 1)
        for a, (real, imag) in enumerate(values):
            out_ref[a % 2, 0, a // 2, rows, :] = real
            out_ref[a % 2, 1, a // 2, rows, :] = imag


def midpoints_kernel(
    q_ref, phase_ref, tw_ref, fh, fl, ih, il, v_ref, work, done, ssem, rsem
):
    core = lax.rem(lax.axis_index("off"), 2)
    j, partner = pair_barrier()

    def piece(i, start):
        rows = pl.ds(pl.multiple_of(i * 32, 32), 32)
        copy = pltpu.make_async_remote_copy(
            done.at[1 - core, :, :, rows],
            v_ref.at[core, :, :, rows],
            ssem.at[i],
            rsem.at[i],
            device_id=(j, partner),
            device_id_type=MESH,
        )
        copy.start() if start else copy.wait()

    def chunk(i, _):
        at = pl.multiple_of(i * 32, 32)
        midpoint_chunk(q_ref, done, phase_ref, tw_ref, (fh, fl), (ih, il), work, at)
        piece(i, True)
        rows = pl.ds(at, 32)
        v_ref[core, :, :, rows] = done[core, :, :, rows]
        return 0

    lax.fori_loop(0, 4, chunk, 0)

    def finish(i, _):
        piece(i, False)
        return 0

    lax.fori_loop(0, 4, finish, 0)


def space_kernel(
    v_ref, slows_ref, omega_ref, fh, fl, ih, il, q_ref, away, ssem, rsem
):
    core = lax.rem(lax.axis_index("off"), 2)
    j, partner = pair_barrier()
    omega = omega_ref[...]
    copies = []
    for pair in range(MID // 2):
        both = jnp.concatenate(
            [
                jnp.concatenate([v_ref[p, part, 2 * pair + q] for q in range(2)], axis=1)
                for p in range(2)
                for part in range(2)
            ],
            axis=0,
        )
        field = dot_table_left(ih[...], il[...], both)
        turned = []
        for q in range(2):
            turn = 2.0 * DZ * omega * (slows_ref[2 * pair + q, core] - 1.0)
            cos, sin = jnp.cos(turn), jnp.sin(turn)
            lanes = slice(q * 128, (q + 1) * 128)
            out_r, out_i = [], []
            for h in range(8):
                real = field[h * 32 : (h + 1) * 32, lanes]
                imag = field[NH + h * 32 : NH + (h + 1) * 32, lanes]
                c, s = cos[h : h + 1], sin[h : h + 1]
                out_r.append(real * c - imag * s)
                out_i.append(real * s + imag * c)
            turned.append(jnp.concatenate(out_r + out_i, axis=0))
        out = dot_table_left(fh[...], fl[...], jnp.concatenate(turned, axis=1))
        copies += store_waves(out, pair, core, partner, q_ref, away, ssem, rsem)
    for copy in copies:
        copy.wait()


def deliver_kernel(
    q_ref, phase_ref, tw_ref, fh, fl, ih, il, z_ref, work, done, ssem, rsem, lsem
):
    j, o = place_here()
    core = lax.rem(o, 2)
    group = o // 2
    owner = j // 4
    mine = lax.rem(j, 4)
    stays = owner == core
    barrier = pltpu.get_barrier_semaphore()
    for i in range(MID):
        for c in range(2):

            @pl.when(jnp.logical_not(jnp.logical_and(i == j, c == core)))
            def _():
                pl.semaphore_signal(
                    barrier, inc=1, device_id=(i, 2 * group + c), device_id_type=MESH
                )

    pl.semaphore_wait(barrier, 2 * MID - 1)

    def send(i, rows):
        def to(d, _):
            peer = lax.rem(j + d, MID)
            for c in range(2):
                for part in range(2):
                    pltpu.make_async_remote_copy(
                        done.at[c, part, peer, rows],
                        z_ref.at[mine, core, part, c, rows],
                        ssem,
                        rsem,
                        device_id=(peer, 2 * group + owner),
                        device_id_type=MESH,
                    ).start()
            return 0

        lax.fori_loop(1, MID, to, 0)

        @pl.when(jnp.logical_not(stays))
        def _():
            to(0, 0)

        @pl.when(stays)
        def _():
            for c in range(2):
                for part in range(2):
                    pltpu.make_async_copy(
                        done.at[c, part, j, rows], z_ref.at[mine, core, part, c, rows], rsem
                    ).start()

    def chunk(i, _):
        at = pl.multiple_of(i * 32, 32)
        midpoint_chunk(q_ref, done, phase_ref, tw_ref, (fh, fl), (ih, il), work, at)
        send(i, pl.ds(at, 32))
        return 0

    lax.fori_loop(0, 4, chunk, 0)
    wait_bytes(z_ref, rsem)
    wait_bytes(done.at[:, :, pl.ds(0, MID - 1)], ssem)

    @pl.when(jnp.logical_not(stays))
    def _():
        wait_bytes(done.at[:, :, 0], ssem)


def table_specs():
    return [VM] * 6


def midpoints(q, phase, twiddle, fwd, inv, cid):
    return exchange_call(
        midpoints_kernel,
        "midpoints",
        FIELD,
        [pltpu.VMEM((512, 256), F32), pltpu.VMEM(FIELD, F32)],
        cid,
        q,
        phase,
        twiddle,
        *fwd,
        *inv,
    )


def deliver(q, phase, twiddle, fwd, inv, cid):
    args = (q, phase, twiddle, *fwd, *inv)
    return pl.pallas_call(
        deliver_kernel,
        out_shape=jax.ShapeDtypeStruct((4, 2, 2, 2, 128, 128), F32),
        in_specs=[VM] * len(args),
        out_specs=VM,
        scratch_shapes=[
            pltpu.VMEM((512, 256), F32),
            pltpu.VMEM(FIELD, F32),
            pltpu.SemaphoreType.DMA,
            pltpu.SemaphoreType.DMA,
            pltpu.SemaphoreType.DMA,
        ],
        compiler_params=pltpu.CompilerParams(
            collective_id=cid, has_side_effects=True, vmem_limit_bytes=56 << 20
        ),
        name="deliver",
    )(*args)


def last_kernel(z_ref, slow_ref, omega_ref, ih, il, out_ref):
    both = jnp.concatenate(
        [
            jnp.concatenate([z_ref[0, p, part, c] for c in range(2)], axis=1)
            for p in range(2)
            for part in range(2)
        ],
        axis=0,
    )
    field = dot_table_left(ih[...], il[...], both)
    omega = omega_ref[0]
    for c in range(2):
        turn = 2.0 * DZ * omega * (slow_ref[c] - 1.0)
        cos, sin = jnp.cos(turn), jnp.sin(turn)
        lanes = slice(c * 128, (c + 1) * 128)
        for h in range(8):
            rows = slice(h * 32, (h + 1) * 32)
            real, imag = field[rows, lanes], field[NH + h * 32 : NH + (h + 1) * 32, lanes]
            co, si = cos[h : h + 1], sin[h : h + 1]
            out_ref[0, rows, 0, lanes] = real * co - imag * si
            out_ref[0, rows, 1, lanes] = real * si + imag * co


def last(z, slow, omega, inv):
    whole = pl.BlockSpec((512, 512), lambda i: (0, 0))
    return pl.pallas_call(
        last_kernel,
        grid=(4,),
        out_shape=jax.ShapeDtypeStruct((4, NH, 2, 256), F32),
        in_specs=[
            pl.BlockSpec((1, 2, 2, 2, 128, 128), lambda i: (i, 0, 0, 0, 0, 0)),
            pl.BlockSpec((2, 8, 128), lambda i: (0, 0, 0)),
            pl.BlockSpec((1, 8, 128), lambda i: (i, 0, 0)),
            whole,
            whole,
        ],
        out_specs=pl.BlockSpec((1, NH, 2, 256), lambda i: (i, 0, 0, 0)),
        compiler_params=pltpu.CompilerParams(vmem_limit_bytes=40 << 20),
        name="last_offsets",
    )(z, slow, omega, *inv)


def one_way(omega_sq, steps):
    wave = steps.astype(F32) * (math.pi / NM)
    level = omega_sq - wave * wave
    magnitude = jnp.sqrt(level * level + DAMP * DAMP)
    larger = jnp.sqrt(0.5 * (magnitude + jnp.abs(level)))
    smaller = DAMP / (2.0 * larger)
    real = jnp.where(level >= 0, larger, smaller)
    imag = jnp.where(level >= 0, smaller, larger)
    decay = jnp.exp(-DZ * imag)
    return jnp.stack([decay * jnp.cos(DZ * real), decay * jnp.sin(DZ * real)])


def phase_kernel(minus_ref, plus_ref, out_ref):
    def one(k, _):
        for q in range(16):
            low = slice(128 - 8 * q, 256 - 8 * q)
            high = slice(8 * q, 8 * q + 128)
            mr, mi = minus_ref[0, k, :, low], minus_ref[1, k, :, low]
            pr, pi = plus_ref[0, k, :, high], plus_ref[1, k, :, high]
            out_ref[0, k, 8 * q : 8 * q + 8, :] = mr * pr - mi * pi
            out_ref[1, k, 8 * q : 8 * q + 8, :] = mr * pi + mi * pr
        return 0

    lax.fori_loop(0, 16, one, 0)


def phase_table(omega, core):
    shape = (16, 8, 256)
    k = lax.broadcasted_iota(jnp.int32, shape, 0)
    i = lax.broadcasted_iota(jnp.int32, shape, 1)
    x = lax.broadcasted_iota(jnp.int32, shape, 2)
    minus = one_way(omega * omega, k - 8 * core - 2048 + 16 * (x - i))
    plus = one_way(omega * omega, k + 8 * core - 2048 + 16 * (x + i))
    return pl.pallas_call(
        phase_kernel,
        out_shape=jax.ShapeDtypeStruct((2, 16, 128, 128), F32),
        in_specs=[VM] * 2,
        out_specs=VM,
        compiler_params=pltpu.CompilerParams(vmem_limit_bytes=40 << 20),
        name="phase_table",
    )(minus, plus)


def frequency(index):
    return math.pi * (0.1 + 0.8 * (index.astype(F32) + 0.5) / NF)


def local(bins_data, operators, targets, counts, layer_index, slowness):
    j, o = place_here()
    group, core = o // 2, lax.rem(o, 2)
    (forward, inverse), (mid_fwd, mid_inv, twiddle) = offset_tables(), midpoint_tables()
    data = bins_data[0].reshape(8, MID, 2, 2, BLK)
    chunks = jnp.einsum("gjrcm,emn->jgcren", data, operators[0], preferred_element_type=F32)
    chunks = chunks.reshape(MID, OFF, 2, ENT, BLK)

    slot = lax.broadcasted_iota(jnp.int32, (8, NB * ENT), 1)
    spread = jnp.tile(targets, (8, NB))
    live = (slot // ENT == o) & (lax.rem(slot, ENT) < counts[0])
    row = jnp.where(live, spread + 1, 0)

    picks = layer_index[:, :, :, None] == lax.broadcasted_iota(jnp.int32, (1, 1, 1, 16), 3)
    slow = jnp.sum(jnp.where(picks, slowness[:, None, None, :], 0.0), axis=3)
    slow = jnp.broadcast_to(slow.transpose(0, 2, 1)[..., None], (2, 2, 8, 128))

    omega = frequency(group * MID + j)
    received, rows, slows = scatter(chunks, row, slow[0])
    phase = phase_table(omega, core)

    waves = exchange_call(
        to_waves_kernel,
        "to_waves",
        FIELD,
        [
            pltpu.VMEM((512, 512), BF16),
            pltpu.VMEM((512, 512), BF16),
            pltpu.VMEM((2, MID, 128, 128), F32),
        ],
        1,
        *forward,
        rows,
        received,
    )
    spectrum = midpoints(waves, phase, twiddle, mid_fwd, mid_inv, 2)
    waves = exchange_call(
        space_kernel,
        "space",
        FIELD,
        [pltpu.VMEM((2, MID, 128, 128), F32)],
        3,
        spectrum,
        slows,
        jnp.full((8, 128), omega, F32),
        *forward,
        *inverse,
    )
    final = deliver(waves, phase, twiddle, mid_fwd, mid_inv, 4)
    own = frequency(o * 4 + lax.broadcasted_iota(jnp.int32, (4, 8, 128), 0))
    return last(final, slow[1], own, inverse)


def solution(mesh):
    in_specs = (
        P("off", None, None, "mid"),
        P("off", None, None, None),
        P("off", None),
        P("off"),
        P(None, None, "mid"),
        P(),
    )
    out_specs = P("off", None, None, "mid")
    return jax.shard_map(local, mesh=mesh, in_specs=in_specs, out_specs=out_specs, check_vma=False)
```

time: 905 us -> 139 us (0.15); the launches traced: 896 us -> 139 us
  waiting for transfers between devices: 480 us -> 0 us
  matrix products: 150 us -> 0.42 us
  Pallas kernels: 0 us -> 127 us
  local copies, waits for them, and re-layouts: 119 us -> 8.71 us
  blocking collectives: 59.6 us -> 0 us
  other arithmetic: 32.9 us -> 1.64 us
  loops' own time: 24.2 us -> 0 us
  starting transfers between devices: 14.9 us -> 0 us
  between operations: 14.5 us -> 0.9 us
    reduce_scatter x1 -> x0, waiting for transfers between devices: 395 us -> none  [local(): lax.psum_scatter(partial_term, 'off', scatter_dimension=0, tiled=True)]
    dot_general x57 -> x1, matrix products: 150 us -> 0.42 us  [local(): jnp.einsum('gjrcm,emn->jgcren', data, operators[0], preferred_element_typ...]
    pallas_call x0 -> x7, Pallas kernels: none -> 127 us  [the longest x1 43.4 us: scatter(): pl.pallas_call(scatter_kernel, out_shape=[jax.ShapeDtypeStruct((MID, 2, N...]
    all_to_all x3 -> x0, waiting for transfers between devices: 85.4 us -> none  [the longest x2 56.6 us: local(): lax.all_to_all(across, 'mid', split_axis=3, concat_axis=1, tiled=True)]
    all_to_all x2 -> x0, blocking collectives: 59.6 us -> none  [the longest x1 31.7 us: local(): lax.all_to_all(owned, 'off', split_axis=1, concat_axis=0, tiled=True)]
    unnamed x22, local copies, waits for them, and re-layouts: 36.3 us -> 5.65 us
    another operation x1 -> x0, loops' own time: 24.2 us -> none  [local(): partial_term = lax.fori_loop(0, counts[0], add_slot, partial_term)]
    all_to_all x8 -> x0, local copies, waits for them, and re-layouts: 23.6 us -> none  [the longest x3 14.4 us: local(): lax.all_to_all(across, 'mid', split_axis=3, concat_axis=1, tiled=True)]
  transfers between devices with their start and end apart: 4 -> 0, of which waited for: 4 -> 0; matrix products, arithmetic and copies ran while one was open for 0% -> 0% of each run, Pallas kernels for 0% -> 0%
where the time goes in v1:
time: 139 us
  Pallas kernels  127 us (91%)
  local copies, waits for them, and re-layouts  8.71 us (6%)
  other arithmetic  1.64 us (1%)
    pallas_call x1, Pallas kernels, scatter(): pl.pallas_call(scatter_kernel, out_shape=[jax.ShapeDtypeStruct((MID, 2, N...  43.4 us
    pallas_call x1, Pallas kernels, deliver(): pl.pallas_call(deliver_kernel, out_shape=jax.ShapeDtypeStruct((4, 2, 2, 2...  40 us
    pallas_call x3, Pallas kernels, exchange_call(): pl.pallas_call(kernel, out_shape=jax.ShapeDtypeStruct(out, F32), in_specs...  35.8 us
    unnamed x22, local copies, waits for them, and re-layouts  5.65 us
    pallas_call x1, Pallas kernels, last(): pl.pallas_call(last_kernel, grid=(4,), out_shape=jax.ShapeDtypeStruct((4,...  4.24 us
    pallas_call x1, Pallas kernels, phase_table(): pl.pallas_call(phase_kernel, out_shape=jax.ShapeDtypeStruct((2, 16, 128,...  3.97 us

profile of v1, /device:TPU:1, one launch (start us, length us, event | category | flops | bytes accessed | tf_op | source)
XLA Modules:
  0.0 139.1 jit_solution(1847175795750643291)
XLA Ops:
  0.0 0.0 copy-start
  0.0 0.9 reshape_squeeze.3
  0.9 0.1 copy-done
  1.1 0.4 convolution_bitcast_fusion
  1.5 0.0 copy-start.10
  1.5 0.0 copy-start.8
  1.5 0.0 copy-start.9
  1.5 1.2 copy.20
  2.8 0.0 copy-done.10
  2.8 0.1 add.157
  3.6 0.0 copy-done.8
  3.6 0.0 copy-done.9
  3.6 0.2 select_reduce_fusion
  3.8 0.1 broadcast_in_dim.34.slow_ref
  3.8 43.4 %scatter_slots.1 = (f32[8,2,16,16,128]{4,3,2,1,0:T(8,128)S(1)}, s32[16,8,256]{2,1,0:T(8,128)S(1)}, f32[8,2,8,128]{3,2,1,0:T(8,128)S(1)}) custom-call(f32[8,16,2,16,128]{4,3,2,1,0:T(8,128)S(1)} %bitcast.22, s32[8,256]{1,0:T(8,128)S(1)} %fusion.6.row_ref, f32[2,8,128]{2,1,0:T(8,128)S(1)} %broadcast_in_dim.34.slow_ref), custom_call_target="tpu_custom_call" | custom-call | tf_op jit(solution)/shard_map/scatter_slots/pallas_call | solution.py:192
  47.2 0.0 copy-start.3
  47.2 1.3 copy-done.3
  48.5 0.0 copy-start.6
  48.5 0.7 copy-done.6
  49.2 0.0 copy-start.7
  49.2 0.6 copy-done.7
  49.8 9.6 %to_waves.1.q_ref = f32[2,2,8,128,128]{4,3,2,1,0:T(8,128)} custom-call(bf16[512,512]{1,0:T(8,128)(2,1)} %constant.103.clone.high_ref.fh, bf16[512,512]{1,0:T(8,128)(2,1)} %constant.104.clone.low_ref.fl, s32[16,8,256]{2,1,0:T(8,128)} %copy-done.6, f32[8,2,16,16,128]{4,3,2,1,0:T(8,128)} %copy-done.3), custom_call_target="tpu_custom_call" | custom-call | tf_op jit(solution)/shard_map/to_waves/pallas_call | solution.py:267
  59.5 0.7 cosine_multiply_fusion.1
  60.2 0.7 cosine_multiply_fusion
  60.9 4.0 %phase_table.1.phase_ref = f32[2,16,128,128]{3,2,1,0:T(8,128)S(1)} custom-call(f32[2,16,8,256]{3,2,1,0:T(8,128)S(1)} %pad_maximum_fusion.minus_ref, f32[2,16,8,256]{3,2,1,0:T(8,128)S(1)} %pad_maximum_fusion.1.plus_ref), custom_call_target="tpu_custom_call" | custom-call | tf_op jit(solution)/shard_map/phase_table/pallas_call | solution.py:570
  64.9 0.0 copy-start.1
  64.9 1.3 copy-done.1
  66.2 13.5 %midpoints.1.v_ref = f32[2,2,8,128,128]{4,3,2,1,0:T(8,128)} custom-call(f32[2,2,8,128,128]{4,3,2,1,0:T(8,128)} %to_waves.1.q_ref, f32[2,16,128,128]{3,2,1,0:T(8,128)} %copy-done.1, f32[16,2,8,128]{3,2,1,0:T(8,128)} %constant.105.clone.tw_ref, bf16[256,256]{1,0:T(8,128)(2,1)} %constant.106.clone.fh, bf16[256,256]{1,0:T(8,128)(2,1)} %constant.107.clone.fl, ...), custom_call_target="tpu_custom_call" | custom-call | tf_op jit(solution)/shard_map/midpoints/pallas_call | solution.py:267
  79.7 0.6 broadcast_in_dim.35.omega_ref
  80.3 12.7 %space.1.q_ref = f32[2,2,8,128,128]{4,3,2,1,0:T(8,128)} custom-call(f32[2,2,8,128,128]{4,3,2,1,0:T(8,128)} %midpoints.1.v_ref, f32[8,2,8,128]{3,2,1,0:T(8,128)} %copy-done.7, f32[8,128]{1,0:T(8,128)} %broadcast_in_dim.35.omega_ref, bf16[512,512]{1,0:T(8,128)(2,1)} %constant.103.clone.high_ref.fh, bf16[512,512]{1,0:T(8,128)(2,1)} %constant.104.clone.low_ref.fl, ...), custom_call_target="tpu_custom_call" | custom-call | tf_op jit(solution)/shard_map/space/pallas_call | solution.py:267
  93.0 0.0 copy-start.4
  93.0 0.0 copy-start.5
  93.0 40.0 %deliver.1.z_ref = f32[4,2,2,2,128,128]{5,4,3,2,1,0:T(8,128)} custom-call(f32[2,2,8,128,128]{4,3,2,1,0:T(8,128)} %space.1.q_ref, f32[2,16,128,128]{3,2,1,0:T(8,128)} %copy-done.1, f32[16,2,8,128]{3,2,1,0:T(8,128)} %constant.105.clone.tw_ref, bf16[256,256]{1,0:T(8,128)(2,1)} %constant.106.clone.fh, bf16[256,256]{1,0:T(8,128)(2,1)} %constant.107.clone.fl, ...), custom_call_target="tpu_custom_call" | custom-call | tf_op jit(solution)/shard_map/deliver/pallas_call | solution.py:476
  133.1 0.1 broadcast_in_dim.37.slow_ref
  133.2 0.1 iota.71.omega_ref
  133.2 0.0 copy-done.4
  133.2 0.0 copy-done.5
  133.2 0.0 copy-start.2
  133.2 1.6 %copy-done.2 = f32[4,2,2,2,128,128]{5,4,3,2,1,0:T(8,128)S(1)} copy-done((f32[4,2,2,2,128,128]{5,4,3,2,1,0:T(8,128)S(1)}, f32[4,2,2,2,128,128]{5,4,3,2,1,0:T(8,128)}, u32[]{:S(2)}) %copy-start.2) | copy-done | bytes 2097176
  134.8 4.2 %last_offsets.1 = f32[4,256,2,256]{3,2,1,0:T(2,128)} custom-call(f32[4,2,2,2,128,128]{5,4,3,2,1,0:T(8,128)S(1)} %copy-done.2, f32[2,8,128]{2,1,0:T(8,128)S(1)} %broadcast_in_dim.37.slow_ref, f32[4,8,128]{2,1,0:T(8,128)S(1)} %iota.71.omega_ref, bf16[512,512]{1,0:T(8,128)(2,1)S(1)} %copy-done.4, bf16[512,512]{1,0:T(8,128)(2,1)S(1)} %copy-done.5), custom_call_target="tpu_custom_call" | custom-call | tf_op jit(solution)/shard_map/last_offsets/pallas_call | solution.py:520
  (10 shorter events, 0.1 us)
Async XLA Ops:
  0.0 1.1 copy-start
  1.5 1.3 copy-start.10
  1.5 2.1 %copy-start.8 = (s32[2,8,2]{1,2,0:T(2,128)S(1)}, s32[2,8,2]{1,2,0:T(2,128)}, u32[]{:S(2)}) copy-start(s32[2,8,2]{1,2,0:T(2,128)} %param.19) | copy-start | bytes 388
  1.5 2.1 %copy-start.9 = (f32[2,16]{1,0:T(2,128)S(1)}, f32[2,16]{1,0:T(2,128)}, u32[]{:S(2)}) copy-start(f32[2,16]{1,0:T(2,128)} %param.20) | copy-start | bytes 388
  47.2 1.3 copy-start.3
  48.5 0.7 copy-start.6
  49.2 0.6 copy-start.7
  64.9 1.3 copy-start.1
  93.0 40.2 %copy-start.4 = (bf16[512,512]{1,0:T(8,128)(2,1)S(1)}, bf16[512,512]{1,0:T(8,128)(2,1)}, u32[]{:S(2)}) copy-start(bf16[512,512]{1,0:T(8,128)(2,1)} %constant.110.clone.ih) | copy-start | bytes 1572868
  93.0 40.2 %copy-start.5 = (bf16[512,512]{1,0:T(8,128)(2,1)S(1)}, bf16[512,512]{1,0:T(8,128)(2,1)}, u32[]{:S(2)}) copy-start(bf16[512,512]{1,0:T(8,128)(2,1)} %constant.111.clone.il) | copy-start | bytes 1572868
  133.2 1.6 %copy-start.2 = (f32[4,2,2,2,128,128]{5,4,3,2,1,0:T(8,128)S(1)}, f32[4,2,2,2,128,128]{5,4,3,2,1,0:T(8,128)}, u32[]{:S(2)}) copy-start(f32[4,2,2,2,128,128]{5,4,3,2,1,0:T(8,128)} %deliver.1.z_ref) | copy-start | bytes 6291460

commit v2 on v0

v2 whole, which is shorter than its diff:
```python
import functools
import math

import jax
import jax.numpy as jnp
import numpy as np
from jax import lax
from jax.experimental import pallas as pl
from jax.experimental.pallas import tpu as pltpu
from jax.sharding import PartitionSpec as P


NF = 64
NH = 256
NM = 2048
BLK = 128
ENT = 16
NB = 16
MID = 8
OFF = 16
DZ = 2.0
DAMP = 0.1
MESH = pl.DeviceIdType.MESH
LEVELS = 32767.0
VM = pl.BlockSpec(memory_space=pltpu.VMEM)
F32 = jnp.float32
BF16 = jnp.bfloat16


def halves(table):
    high = np.asarray(table, np.float32).astype(jnp.bfloat16)
    low = (np.asarray(table, np.float64) - high.astype(np.float64)).astype(np.float32)
    return high, low.astype(jnp.bfloat16)


def offset_tables():
    forward, inverse = [], []
    place = np.arange(128)
    for p in range(2):
        wave = 2 * (np.arange(128) - 64) + p
        angle = 2.0 * np.pi * (np.outer(wave, place) % NH) / NH
        cos, sin = np.cos(angle), np.sin(angle)
        forward.append(np.block([[cos, sin], [-sin, cos]]))
        inverse.append(np.block([[cos.T, -sin.T], [sin.T, cos.T]]) / NH)
    return halves(np.stack(forward)), halves(np.stack(inverse))


def midpoint_tables():
    inner = np.arange(128)
    wave = (np.arange(128) + 64) % 128
    angle = 2.0 * np.pi * (np.outer(inner, wave) % 128) / 128
    cos, sin = np.cos(angle), np.sin(angle)
    forward = np.block([[cos, -sin], [sin, cos]])
    inverse = np.block([[cos.T, sin.T], [-sin.T, cos.T]]) / NM
    turn = 2.0 * np.pi * np.outer(np.arange(16), inner) / NM
    twiddle = np.stack([np.cos(turn), np.sin(turn)], 1)
    twiddle = np.broadcast_to(twiddle[:, :, None], (16, 2, 8, 128)).astype(np.float32)
    return halves(forward), halves(inverse), np.ascontiguousarray(twiddle)


def split(x):
    high = x.astype(BF16)
    return high, (x - high.astype(F32)).astype(BF16)


def dot(a, b):
    return jnp.dot(a, b, preferred_element_type=F32)


def dot_table_left(high, low, x):
    x_high, x_low = split(x)
    return dot(high, x_high) + (dot(high, x_low) + dot(low, x_high))


def dot_table_right(x, high, low):
    x_high, x_low = split(x)
    return dot(x_high, high) + (dot(x_low, high) + dot(x_high, low))


def times_root(value, step, sign):
    real, imag = value
    step = step % 16
    if step == 0:
        return value
    if step == 4:
        return (-imag * sign, real * sign)
    half = float(np.sqrt(0.5))
    if step == 2:
        return ((real - sign * imag) * half, (imag + sign * real) * half)
    if step == 6:
        return ((-real - sign * imag) * half, (-imag + sign * real) * half)
    c, s = math.cos(2 * math.pi * step / 16), sign * math.sin(2 * math.pi * step / 16)
    return (real * c - imag * s, real * s + imag * c)


def small_fft(values, sign):
    n = len(values)
    if n == 1:
        return values
    even, odd = small_fft(values[0::2], sign), small_fft(values[1::2], sign)
    odd = [times_root(v, k * (16 // n), sign) for k, v in enumerate(odd)]
    return [(e[0] + o[0], e[1] + o[1]) for e, o in zip(even, odd)] + [
        (e[0] - o[0], e[1] - o[1]) for e, o in zip(even, odd)
    ]


def place_here():
    return lax.axis_index("mid"), lax.axis_index("off")


def wait_bytes(ref, sem):
    pltpu.make_async_copy(ref, ref, sem).wait()


def code(values, peak):
    return jnp.round(values * (LEVELS / peak)).astype(jnp.int32).astype(jnp.int16)


def decode(codes, scale):
    return codes.astype(jnp.int32).astype(F32) * scale


def peak_of(arrays):
    top = functools.reduce(jnp.maximum, [jnp.abs(a) for a in arrays])
    return jnp.maximum(jnp.max(top, axis=0, keepdims=True), 1e-30)


def one_way(omega_sq, steps):
    wave = steps.astype(F32) * (math.pi / NM)
    level = omega_sq - wave * wave
    magnitude = jnp.sqrt(level * level + DAMP * DAMP)
    larger = jnp.sqrt(0.5 * (magnitude + jnp.abs(level)))
    smaller = DAMP / (2.0 * larger)
    real = jnp.where(level >= 0, larger, smaller)
    imag = jnp.where(level >= 0, smaller, larger)
    decay = jnp.exp(-DZ * imag)
    return decay * jnp.cos(DZ * real), decay * jnp.sin(DZ * real)


def frequency(index):
    return math.pi * (0.1 + 0.8 * (index.astype(F32) + 0.5) / NF)


def fill_phase(phase, omega, core):
    shape = (8, 256)
    i = lax.broadcasted_iota(jnp.int32, shape, 0)
    x = lax.broadcasted_iota(jnp.int32, shape, 1)
    omega_sq = omega * omega

    def one(k, _):
        mr, mi = one_way(omega_sq, k - 8 * core - NM + 16 * (x - i))
        pr, pi = one_way(omega_sq, k + 8 * core - NM + 16 * (x + i))
        for q in range(16):
            low = slice(128 - 8 * q, 256 - 8 * q)
            high = slice(8 * q, 8 * q + 128)
            ar, ai, br, bi = mr[:, low], mi[:, low], pr[:, high], pi[:, high]
            phase[0, k, 8 * q : 8 * q + 8, :] = ar * br - ai * bi
            phase[1, k, 8 * q : 8 * q + 8, :] = ar * bi + ai * br
        return 0

    lax.fori_loop(0, 16, one, 0)


def midpoint_chunk(x_ref, core, store, phase, tw_ref, fwd, inv, work, at):
    for sub in range(4):
        rows = pl.ds(at + sub * 8, 8)
        values = [
            (x_ref[a % 2, core, 0, a // 2, rows, :], x_ref[a % 2, core, 1, a // 2, rows, :])
            for a in range(16)
        ]
        for k, (real, imag) in enumerate(small_fft(values, -1)):
            cos, sin = tw_ref[k, 0], tw_ref[k, 1]
            here = pl.ds(k * 32 + sub * 8, 8)
            work[here, 0:128] = real * cos + imag * sin
            work[here, 128:256] = imag * cos - real * sin
    for part in range(4):
        here = pl.ds(part * 128, 128)
        z = dot_table_right(work[here, :], fwd[0][...], fwd[1][...])
        real, imag = z[:, :128], z[:, 128:]
        ks = pl.ds(part * 4, 4)
        turn_r = phase[0, ks, pl.ds(at, 32), :].reshape(128, 128)
        turn_i = phase[1, ks, pl.ds(at, 32), :].reshape(128, 128)
        z = jnp.concatenate(
            [real * turn_r - imag * turn_i, real * turn_i + imag * turn_r], axis=1
        )
        work[here, :] = dot_table_right(z, inv[0][...], inv[1][...])
    for sub in range(4):
        values = []
        for k in range(16):
            here = pl.ds(k * 32 + sub * 8, 8)
            real, imag = work[here, 0:128], work[here, 128:256]
            cos, sin = tw_ref[k, 0], tw_ref[k, 1]
            values.append((real * cos - imag * sin, real * sin + imag * cos))
        store(sub, small_fft(values, 1))


def field_kernel(
    bins_ref,
    ops_ref,
    row_ref,
    slow_ref,
    oh_ref,
    ol_ref,
    gh_ref,
    gl_ref,
    fh,
    fl,
    ih,
    il,
    tw_ref,
    z_ref,
    zs_ref,
    made,
    sent,
    sent_s,
    held,
    held_s,
    rows,
    slows,
    turns,
    phase,
    w_high,
    w_low,
    x0,
    d0,
    x1,
    work,
    chunk_out,
    coded,
    coded_s,
    ssem,
    rsem,
    msem,
    pair_s,
    pair_r,
):
    j, o = place_here()
    core, group = lax.rem(o, 2), o // 2
    partner = o + 1 - 2 * core
    me, total = j * OFF + o, MID * OFF
    barrier = pltpu.get_barrier_semaphore()

    def signal(i, _):
        peer = lax.rem(me + i, total)
        pl.semaphore_signal(
            barrier, inc=1, device_id=(peer // OFF, lax.rem(peer, OFF)), device_id_type=MESH
        )
        return 0

    lax.fori_loop(1, total, signal, 0)

    for c in range(2):
        source = bins_ref[c].reshape(2 * NF, BLK)
        for e in range(0, ENT, 2):
            out = dot(source, jnp.concatenate([ops_ref[e], ops_ref[e + 1]], axis=1))
            made[c, pl.ds(e * 128, 128), :] = out[:, :BLK]
            made[c, pl.ds(e * 128 + 128, 128), :] = out[:, BLK:]

    pl.semaphore_wait(barrier, total - 1)

    pltpu.make_async_copy(row_ref, rows.at[o], msem.at[0]).start()
    pltpu.make_async_copy(slow_ref, slows.at[j], msem.at[1]).start()

    def send_row(i, _):
        peer = lax.rem(o + i, OFF)
        pltpu.make_async_remote_copy(
            row_ref, rows.at[o], msem.at[2], msem.at[0], device_id=(j, peer), device_id_type=MESH
        ).start()
        return 0

    lax.fori_loop(1, OFF, send_row, 0)

    def send_slow(i, _):
        peer = lax.rem(j + i, MID)
        pltpu.make_async_remote_copy(
            slow_ref, slows.at[j], msem.at[3], msem.at[1], device_id=(peer, o), device_id_type=MESH
        ).start()
        return 0

    lax.fori_loop(1, MID, send_slow, 0)

    def peer_at(i):
        at = lax.rem(i * 45, total)
        return lax.rem(j + at // OFF, MID), lax.rem(o + lax.rem(at, OFF), OFF)

    def encode(i):
        peer_j, peer_o = peer_at(i)
        f, c = 8 * (peer_o // 2) + peer_j, lax.rem(peer_o, 2)
        values = [made[c, pl.ds(part * NF + f, ENT, stride=2 * NF), :] for part in range(2)]
        peak = peak_of(values)
        for part in range(2):
            sent[peer_j, peer_o, part] = code(values[part], peak)
        sent_s[peer_j, peer_o] = peak * (1.0 / LEVELS)

    def send(i):
        peer_j, peer_o = peer_at(i)
        for source, target, at in ((sent, held, 0), (sent_s, held_s, 1)):
            pltpu.make_async_remote_copy(
                source.at[peer_j, peer_o],
                target.at[j, o],
                ssem.at[at],
                rsem.at[at],
                device_id=(peer_j, peer_o),
                device_id_type=MESH,
            ).start()

    encode(0)
    encode(1)

    def go(i, _):
        encode(i)
        send(i - 1)
        return 0

    lax.fori_loop(2, total, go, 0)
    send(total - 1)
    pltpu.make_async_copy(sent.at[j, o], held.at[j, o], rsem.at[0]).start()
    pltpu.make_async_copy(sent_s.at[j, o], held_s.at[j, o], rsem.at[1]).start()

    own_f = lax.broadcasted_iota(jnp.int32, (8, 128), 0) * 0 + (group * MID + j)
    omega = frequency(own_f)
    fill_phase(phase, jnp.concatenate([omega, omega], axis=1), core)
    wait_bytes(slows, msem.at[1])
    for jm in range(MID):
        turn = 2.0 * DZ * omega * (slows[jm, core] - 1.0)
        turns[jm, 0] = jnp.cos(turn)
        turns[jm, 1] = jnp.sin(turn)
    wait_bytes(rows, msem.at[0])
    target = jnp.sum(rows[:, 0, :], axis=0, keepdims=True) - 1
    spot = lax.broadcasted_iota(jnp.int32, (128, NB * ENT), 0)
    first, second = (spot == target).astype(F32), (spot + 128 == target).astype(F32)
    for p in range(2):
        pick = ((first + second) if p == 0 else (first - second)).astype(BF16)
        for part in range(2):
            cols = pl.ds(part * 128, 128)
            at = pl.ds(part * NH, NH)
            w_high[p, :, at] = dot(oh_ref[p, :, cols], pick).astype(BF16)
            w_low[p, :, at] = dot(ol_ref[p, :, cols], pick).astype(BF16)
    wait_bytes(rows.at[pl.ds(0, OFF - 1)], msem.at[2])
    wait_bytes(slows.at[pl.ds(0, MID - 1)], msem.at[3])
    wait_bytes(held_s, rsem.at[1])
    wait_bytes(held, rsem.at[0])

    def pair_copy(ref, pair, step):
        here = ref.at[core, 1 - core, :, pl.ds(2 * pair, 2)]
        return pltpu.make_async_remote_copy(
            here,
            here,
            pair_s.at[step, pair],
            pair_r.at[step, pair],
            device_id=(j, partner),
            device_id_type=MESH,
        )

    def put_waves(ref, pair, p, out):
        for q in range(2):
            for part in range(2):
                ref[core, p, part, 2 * pair + q] = out[
                    part * 128 : (part + 1) * 128, q * 128 : (q + 1) * 128
                ]

    def to_waves(pair, _):
        both = jnp.concatenate(
            [
                jnp.concatenate(
                    [
                        decode(held[2 * pair + q, :, part], held_s[2 * pair + q]).reshape(
                            NB * ENT, 128
                        )
                        for q in range(2)
                    ],
                    axis=1,
                )
                for part in range(2)
            ],
            axis=0,
        )
        for p in range(2):
            put_waves(x0, pair, p, dot_table_left(w_high[p], w_low[p], both))
        pair_copy(x0, pair, 0).start()
        return 0

    lax.fori_loop(0, MID // 2, to_waves, 0)
    for pair in range(MID // 2):
        pair_copy(x0, pair, 0).wait_recv()

    def chunk_copy(i):
        here = d0.at[core, 1 - core, :, :, pl.ds(pl.multiple_of(i * 32, 32), 32)]
        return pltpu.make_async_remote_copy(
            here,
            here,
            pair_s.at[1, i],
            pair_r.at[1, i],
            device_id=(j, partner),
            device_id_type=MESH,
        )

    def first_chunk(i, _):
        at = pl.multiple_of(i * 32, 32)

        def store(sub, values):
            rows_here = pl.ds(at + sub * 8, 8)
            for a, (real, imag) in enumerate(values):
                d0[core, a % 2, 0, a // 2, rows_here, :] = real
                d0[core, a % 2, 1, a // 2, rows_here, :] = imag

        midpoint_chunk(x0, core, store, phase, tw_ref, (fh, fl), (ih, il), work, at)
        chunk_copy(i).start()
        return 0

    lax.fori_loop(0, 4, first_chunk, 0)
    for i in range(4):
        chunk_copy(i).wait_recv()

    def space(pair, _):
        fields = []
        for p in range(2):
            both = jnp.concatenate(
                [
                    jnp.concatenate([d0[p, core, part, 2 * pair + q] for q in range(2)], axis=1)
                    for part in range(2)
                ],
                axis=0,
            )
            fields.append(dot_table_left(gh_ref[p], gl_ref[p], both))
        ends = [fields[0] + fields[1], fields[0] - fields[1]]
        for end in range(2):
            turned = []
            for q in range(2):
                cos, sin = turns[2 * pair + q, 0], turns[2 * pair + q, 1]
                lanes = slice(q * 128, (q + 1) * 128)
                out_r, out_i = [], []
                for h in range(4):
                    real = ends[end][h * 32 : (h + 1) * 32, lanes]
                    imag = ends[end][128 + h * 32 : 128 + (h + 1) * 32, lanes]
                    at = 4 * end + h
                    c, s = cos[at : at + 1], sin[at : at + 1]
                    out_r.append(real * c - imag * s)
                    out_i.append(real * s + imag * c)
                turned.append(jnp.concatenate(out_r + out_i, axis=0))
            ends[end] = jnp.concatenate(turned, axis=1)
        folded = (ends[0] + ends[1], ends[0] - ends[1])
        for p in range(2):
            put_waves(x1, pair, p, dot_table_left(oh_ref[p], ol_ref[p], folded[p]))
        pair_copy(x1, pair, 2).start()
        return 0

    lax.fori_loop(0, MID // 2, space, 0)
    for pair in range(MID // 2):
        pair_copy(x1, pair, 2).wait_recv()

    owner, mine = j // 4, lax.rem(j, 4)
    stays = owner == core
    x_at, y_at = j // 2, lax.rem(j, 2)

    def deliver(peer, i, near):
        for source, target, at in ((coded, z_ref, 2), (coded_s, zs_ref, 3)):
            here, there = source.at[peer, i], target.at[mine, core, i]
            if near:
                pltpu.make_async_copy(here, there, rsem.at[at]).start()
            else:
                pltpu.make_async_remote_copy(
                    here,
                    there,
                    ssem.at[at],
                    rsem.at[at],
                    device_id=(peer, 2 * group + owner),
                    device_id_type=MESH,
                ).start()

    def second_chunk(i, _):
        at = pl.multiple_of(i * 32, 32)

        def store(sub, values):
            rows_here = pl.ds(sub * 8, 8)
            for a, (real, imag) in enumerate(values):
                chunk_out[a // 2, a % 2, 0, rows_here, :] = real
                chunk_out[a // 2, a % 2, 1, rows_here, :] = imag

        midpoint_chunk(x1, core, store, phase, tw_ref, (fh, fl), (ih, il), work, at)

        def encode_peer(peer, _):
            for c in range(2):
                values = [chunk_out[peer, c, part] for part in range(2)]
                peak = peak_of(values)
                for part in range(2):
                    coded[peer, i, c, part] = code(values[part], peak)
                coded_s[peer, i, c] = peak * (1.0 / LEVELS)
            return 0

        lax.fori_loop(0, MID, encode_peer, 0)
        for dx, dy in ((1, 0), (0, 1), (3, 0), (2, 1), (1, 1), (2, 0), (3, 1)):
            peer = 2 * lax.rem(x_at + dx, 4) + lax.rem(y_at + dy, 2)
            deliver(peer, i, False)

        @pl.when(stays)
        def _():
            deliver(j, i, True)

        @pl.when(jnp.logical_not(stays))
        def _():
            deliver(j, i, False)

        return 0

    lax.fori_loop(0, 4, second_chunk, 0)

    for at, ref in ((0, sent), (1, sent_s)):
        wait_bytes(ref.at[0, pl.ds(0, OFF - 1)], ssem.at[at])
        wait_bytes(ref.at[pl.ds(1, MID - 1)], ssem.at[at])
    for i in range(4):
        pair_copy(x0, i, 0).wait_send()
        chunk_copy(i).wait_send()
        pair_copy(x1, i, 2).wait_send()
    for at, ref in ((2, coded), (3, coded_s)):
        wait_bytes(ref.at[pl.ds(0, MID - 1)], ssem.at[at])

        @pl.when(jnp.logical_not(stays))
        def _():
            wait_bytes(ref.at[0], ssem.at[at])

    wait_bytes(zs_ref, rsem.at[3])
    wait_bytes(z_ref, rsem.at[2])


HALVES = (2, 2, 2, MID, 128, 128)


def propagate(*args):
    return pl.pallas_call(
        field_kernel,
        out_shape=[
            jax.ShapeDtypeStruct((4, 2, 4, 2, 2, 32, 128), jnp.int16),
            jax.ShapeDtypeStruct((4, 2, 4, 2, 1, 128), F32),
        ],
        in_specs=[VM] * len(args),
        out_specs=[VM] * 2,
        scratch_shapes=[
            pltpu.VMEM((2, ENT * 2 * NF, BLK), F32),
            pltpu.VMEM((MID, OFF, 2, ENT, BLK), jnp.int16),
            pltpu.VMEM((MID, OFF, 1, BLK), F32),
            pltpu.VMEM((MID, NB, 2, ENT, BLK), jnp.int16),
            pltpu.VMEM((MID, NB, 1, BLK), F32),
            pltpu.VMEM((NB, 8, NB * ENT), jnp.int32),
            pltpu.VMEM((MID, 2, 8, 128), F32),
            pltpu.VMEM((MID, 2, 8, 128), F32),
            pltpu.VMEM((2, 16, 128, 128), F32),
            pltpu.VMEM((2, 256, 512), BF16),
            pltpu.VMEM((2, 256, 512), BF16),
            pltpu.VMEM(HALVES, F32),
            pltpu.VMEM(HALVES, F32),
            pltpu.VMEM(HALVES, F32),
            pltpu.VMEM((512, 256), F32),
            pltpu.VMEM((MID, 2, 2, 32, 128), F32),
            pltpu.VMEM((MID, 4, 2, 2, 32, 128), jnp.int16),
            pltpu.VMEM((MID, 4, 2, 1, 128), F32),
            pltpu.SemaphoreType.DMA((4,)),
            pltpu.SemaphoreType.DMA((4,)),
            pltpu.SemaphoreType.DMA((4,)),
            pltpu.SemaphoreType.DMA((3, 4)),
            pltpu.SemaphoreType.DMA((3, 4)),
        ],
        compiler_params=pltpu.CompilerParams(
            collective_id=0, has_side_effects=True, vmem_limit_bytes=56 << 20
        ),
        name="propagate",
    )(*args)


def last_kernel(z_ref, zs_ref, slow_ref, omega_ref, gh_ref, gl_ref, out_ref):
    fields = []
    for p in range(2):
        both = jnp.concatenate(
            [
                jnp.concatenate(
                    [decode(z_ref[0, p, q, c, part], zs_ref[0, p, q, c]) for c in range(2)],
                    axis=1,
                )
                for part in range(2)
                for q in range(4)
            ],
            axis=0,
        )
        fields.append(dot_table_left(gh_ref[p], gl_ref[p], both))
    ends = [fields[0] + fields[1], fields[0] - fields[1]]
    omega = omega_ref[0]
    for c in range(2):
        turn = 2.0 * DZ * omega * (slow_ref[c] - 1.0)
        cos, sin = jnp.cos(turn), jnp.sin(turn)
        lanes = slice(c * 128, (c + 1) * 128)
        for h in range(8):
            end, at = ends[h // 4], (h % 4) * 32
            rows = slice(h * 32, (h + 1) * 32)
            real, imag = end[at : at + 32, lanes], end[128 + at : 160 + at, lanes]
            co, si = cos[h : h + 1], sin[h : h + 1]
            out_ref[0, rows, 0, lanes] = real * co - imag * si
            out_ref[0, rows, 1, lanes] = real * si + imag * co


def last(z, zs, slow, omega, inv):
    whole = pl.BlockSpec((2, 256, 256), lambda i: (0, 0, 0))
    return pl.pallas_call(
        last_kernel,
        grid=(4,),
        out_shape=jax.ShapeDtypeStruct((4, NH, 2, 256), F32),
        in_specs=[
            pl.BlockSpec((1, 2, 4, 2, 2, 32, 128), lambda i: (i, 0, 0, 0, 0, 0, 0)),
            pl.BlockSpec((1, 2, 4, 2, 1, 128), lambda i: (i, 0, 0, 0, 0, 0)),
            pl.BlockSpec((2, 8, 128), lambda i: (0, 0, 0)),
            pl.BlockSpec((1, 8, 128), lambda i: (i, 0, 0)),
            whole,
            whole,
        ],
        out_specs=pl.BlockSpec((1, NH, 2, 256), lambda i: (i, 0, 0, 0)),
        compiler_params=pltpu.CompilerParams(vmem_limit_bytes=40 << 20),
        name="last_offsets",
    )(z, zs, slow, omega, *inv)


def local(bins_data, operators, targets, counts, layer_index, slowness):
    j, o = place_here()
    (forward, inverse), (mid_fwd, mid_inv, twiddle) = offset_tables(), midpoint_tables()
    bins = bins_data[0].reshape(NF, 2, 2, BLK).transpose(2, 1, 0, 3)

    slot = lax.broadcasted_iota(jnp.int32, (8, NB * ENT), 1)
    spread = jnp.tile(targets, (8, NB))
    live = (slot // ENT == o) & (lax.rem(slot, ENT) < counts[0])
    row = jnp.where(live, spread + 1, 0)

    picks = layer_index[:, :, :, None] == lax.broadcasted_iota(jnp.int32, (1, 1, 1, 16), 3)
    slow = jnp.sum(jnp.where(picks, slowness[:, None, None, :], 0.0), axis=3)
    slow = jnp.broadcast_to(slow.transpose(0, 2, 1)[..., None], (2, 2, 8, 128))

    z, zs = propagate(
        bins, operators[0], row, slow[0], *forward, *inverse, *mid_fwd, *mid_inv, twiddle
    )
    own = frequency(o * 4 + lax.broadcasted_iota(jnp.int32, (4, 8, 128), 0))
    return last(z, zs, slow[1], own, inverse)


def solution(mesh):
    in_specs = (
        P("off", None, None, "mid"),
        P("off", None, None, None),
        P("off", None),
        P("off"),
        P(None, None, "mid"),
        P(),
    )
    out_specs = P("off", None, None, "mid")
    return jax.shard_map(local, mesh=mesh, in_specs=in_specs, out_specs=out_specs, check_vma=False)
```

time: 905 us -> 72.2 us (0.08)
  waiting for transfers between devices: 480 us -> 0 us
  matrix products: 150 us -> 0 us
  local copies, waits for them, and re-layouts: 119 us -> 4.4 us
  Pallas kernels: 0 us -> 64.6 us
  blocking collectives: 59.6 us -> 0 us
  other arithmetic: 32.9 us -> 2.14 us
  loops' own time: 24.2 us -> 0 us
  starting transfers between devices: 14.9 us -> 0 us
  between operations: 14.5 us -> 0.76 us
    reduce_scatter x1 -> x0, waiting for transfers between devices: 395 us -> none  [local(): lax.psum_scatter(partial_term, 'off', scatter_dimension=0, tiled=True)]
    dot_general x57 -> x0, matrix products: 150 us -> none  [the longest x48 142 us: contract(): jnp.einsum(form, left, right, precision=lax.Precision.HIGHEST, preferred_...]
    all_to_all x3 -> x0, waiting for transfers between devices: 85.4 us -> none  [the longest x2 56.6 us: local(): lax.all_to_all(across, 'mid', split_axis=3, concat_axis=1, tiled=True)]
    pallas_call x0 -> x2, Pallas kernels: none -> 64.6 us  [the longest x1 60.9 us: propagate(): pl.pallas_call(field_kernel, out_shape=[jax.ShapeDtypeStruct((4, 2, 4, 2,...]
    all_to_all x2 -> x0, blocking collectives: 59.6 us -> none  [the longest x1 31.7 us: local(): lax.all_to_all(owned, 'off', split_axis=1, concat_axis=0, tiled=True)]
    unnamed x22 -> x8, local copies, waits for them, and re-layouts: 36.3 us -> 1.98 us
    another operation x1 -> x0, loops' own time: 24.2 us -> none  [local(): partial_term = lax.fori_loop(0, counts[0], add_slot, partial_term)]
    all_to_all x8 -> x0, local copies, waits for them, and re-layouts: 23.6 us -> none  [the longest x3 14.4 us: local(): lax.all_to_all(across, 'mid', split_axis=3, concat_axis=1, tiled=True)]
  transfers between devices with their start and end apart: 4 -> 0, of which waited for: 4 -> 0; matrix products, arithmetic and copies ran while one was open for 0% -> 0% of each run, Pallas kernels for 0% -> 0%
where the time goes in v2:
time: 72.2 us; the launch traced here: 71.9 us
  Pallas kernels  64.6 us (89%)
  local copies, waits for them, and re-layouts  4.4 us (6%)
  other arithmetic  2.14 us (3%)
  between operations  0.76 us (1%)
    pallas_call x1, Pallas kernels, propagate(): pl.pallas_call(field_kernel, out_shape=[jax.ShapeDtypeStruct((4, 2, 4, 2,...  60.9 us
    pallas_call x1, Pallas kernels, last(): pl.pallas_call(last_kernel, grid=(4,), out_shape=jax.ShapeDtypeStruct((4,...  3.7 us
    unnamed x8, local copies, waits for them, and re-layouts  1.98 us
    another operation x2, local copies, waits for them, and re-layouts, local(): bins = bins_data[0].reshape(NF, 2, 2, BLK).transpose(2, 1, 0, 3)  1.53 us

profile of v2, /device:TPU:1, one launch (start us, length us, event | category | flops | bytes accessed | tf_op | source)
XLA Modules:
  0.0 71.9 jit_solution(10488915113821925842)
XLA Ops:
  0.0 0.0 copy-start
  0.0 0.0 copy-start.1
  0.7 0.7 add_bitcast_fusion
  1.4 0.9 %select_reduce_fusion = f32[2,8,2]{1,2,0:T(2,128)S(1)} fusion(f32[2,16]{1,0:T(2,128)} %param.20, s32[2,8,2]{1,2,0:T(2,128)} %param.19), kind=kLoop, calls=%fused_computation.1 | loop fusion | flops 1504 | bytes 384 | tf_op jit(solution)/shard_map/reduce_sum | solution.py:631
  2.3 0.1 broadcast_in_dim.33.slow_ref
  2.3 0.1 add.37
  2.4 0.6 fusion.1.row_ref
  3.0 0.7 broadcast_in_dim.31.slow_ref
  3.7 0.1 iota.31.omega_ref
  3.8 0.9 %reshape.15 = bf16[64,2,2,128]{3,2,1,0:T(2,128)(2,1)S(1)} reshape(bf16[1,64,2,256]{3,2,1,0:T(2,128)(2,1)} %param.15) | data formatting | bytes 131072 | tf_op jit(solution)/shard_map/reshape;squeeze | solution.py:623
  4.6 0.6 copy.25
  5.3 60.9 %propagate.1 = (s16[4,2,4,2,2,32,128]{6,5,4,3,2,1,0:T(8,128)(2,1)}, f32[4,2,4,2,1,128]{5,4,3,2,1,0:T(1,128)}) custom-call(bf16[2,2,64,128]{3,2,1,0:T(8,128)(2,1)} %bitcast.14, bf16[16,128,128]{2,1,0:T(8,128)(2,1)} %bitcast.13, s32[8,256]{1,0:T(8,128)} %fusion.1.row_ref, f32[2,8,128]{2,1,0:T(8,128)} %broadcast_in_dim.31.slow_ref, ...), custom_call_target="tpu_custom_call" | custom-call | tf_op jit(solution)/shard_map/propagate/pallas_call | solution.py:530
  66.2 0.0 copy-done
  66.2 0.0 copy-done.1
  66.2 0.0 copy-start.2
  66.2 1.2 %copy-done.2 = s16[4,2,4,2,2,32,128]{6,5,4,3,2,1,0:T(8,128)(2,1)S(1)} copy-done((s16[4,2,4,2,2,32,128]{6,5,4,3,2,1,0:T(8,128)(2,1)S(1)}, s16[4,2,4,2,2,32,128]{6,5,4,3,2,1,0:T(8,128)(2,1)}, u32[]{:S(2)}) %copy-start.2) | copy-done | bytes 1048600
  67.4 0.0 copy-start.3
  67.4 0.8 %copy-done.3 = f32[4,2,4,2,1,128]{5,4,3,2,1,0:T(1,128)S(1)} copy-done((f32[4,2,4,2,1,128]{5,4,3,2,1,0:T(1,128)S(1)}, f32[4,2,4,2,1,128]{5,4,3,2,1,0:T(1,128)}, u32[]{:S(2)}) %copy-start.3) | copy-done | bytes 32792
  68.2 3.7 %last_offsets.1 = f32[4,256,2,256]{3,2,1,0:T(2,128)} custom-call(s16[4,2,4,2,2,32,128]{6,5,4,3,2,1,0:T(8,128)(2,1)S(1)} %copy-done.2, f32[4,2,4,2,1,128]{5,4,3,2,1,0:T(1,128)S(1)} %copy-done.3, f32[2,8,128]{2,1,0:T(8,128)S(1)} %broadcast_in_dim.33.slow_ref, f32[4,8,128]{2,1,0:T(8,128)S(1)} %iota.31.omega_ref, bf16[2,256,256]{2,1,0:T(8,128)(2,1)S(1)} %copy-done.1, ...), custom_call_target="tpu_custom_call" | custom-call | tf_op jit(solution)/shard_map/last_offsets/pallas_call | solution.py:602
  (5 shorter events, 0.0 us)
Async XLA Ops:
  0.0 66.2 %copy-start = (bf16[2,256,256]{2,1,0:T(8,128)(2,1)S(1)}, bf16[2,256,256]{2,1,0:T(8,128)(2,1)}, u32[]{:S(2)}) copy-start(bf16[2,256,256]{2,1,0:T(8,128)(2,1)} %constant.62.clone.gl_ref) | copy-start | bytes 786436
  0.0 66.2 %copy-start.1 = (bf16[2,256,256]{2,1,0:T(8,128)(2,1)S(1)}, bf16[2,256,256]{2,1,0:T(8,128)(2,1)}, u32[]{:S(2)}) copy-start(bf16[2,256,256]{2,1,0:T(8,128)(2,1)} %constant.61.clone.gh_ref) | copy-start | bytes 786436
  66.2 1.2 %copy-start.2 = (s16[4,2,4,2,2,32,128]{6,5,4,3,2,1,0:T(8,128)(2,1)S(1)}, s16[4,2,4,2,2,32,128]{6,5,4,3,2,1,0:T(8,128)(2,1)}, u32[]{:S(2)}) copy-start(s16[4,2,4,2,2,32,128]{6,5,4,3,2,1,0:T(8,128)(2,1)} %get-tuple-element.7.z_ref) | copy-start | bytes 3145732
  67.4 0.8 %copy-start.3 = (f32[4,2,4,2,1,128]{5,4,3,2,1,0:T(1,128)S(1)}, f32[4,2,4,2,1,128]{5,4,3,2,1,0:T(1,128)}, u32[]{:S(2)}) copy-start(f32[4,2,4,2,1,128]{5,4,3,2,1,0:T(1,128)} %get-tuple-element.8.zs_ref) | copy-start | bytes 98308

commit v3 on v2

--- a/solution.py
+++ b/solution.py
@@ -1,4 +1,5 @@
 import functools
+import itertools
 import math
 
 import jax
@@ -23,6 +24,8 @@
 MESH = pl.DeviceIdType.MESH
 LEVELS = 32767.0
 VM = pl.BlockSpec(memory_space=pltpu.VMEM)
+SM = pl.BlockSpec(memory_space=pltpu.SMEM)
+ANY = pl.BlockSpec(memory_space=pl.ANY)
 F32 = jnp.float32
 BF16 = jnp.bfloat16
 
@@ -135,6 +138,14 @@
     imag = jnp.where(level >= 0, smaller, larger)
     decay = jnp.exp(-DZ * imag)
     return decay * jnp.cos(DZ * real), decay * jnp.sin(DZ * real)
+
+
+def slow_tile(layers_ref, slowness_ref, step, c):
+    at = lax.broadcasted_iota(jnp.int32, (8, 128), 0)
+    tile = jnp.zeros((8, 128), F32)
+    for h in range(8):
+        tile = jnp.where(at == h, slowness_ref[step, layers_ref[step, c, h]], tile)
+    return tile
 
 
 def frequency(index):
@@ -195,21 +206,39 @@
 
 
 def field_kernel(
-    bins_ref,
-    ops_ref,
+    targets_ref,
+    counts_ref,
+    layers_ref,
+    slowness_ref,
+    bins_hbm,
+    ops_hbm,
+    *rest,
+):
+    tables_hbm, (z_ref, zs_ref), scratch = rest[:9], rest[9:11], rest[11:]
+    field_body(
+        targets_ref,
+        counts_ref,
+        layers_ref,
+        slowness_ref,
+        (bins_hbm, ops_hbm, *tables_hbm),
+        scratch[:11],
+        z_ref,
+        zs_ref,
+        *scratch[11:],
+    )
+
+
+def field_body(
+    targets_ref,
+    counts_ref,
+    layers_ref,
+    slowness_ref,
+    held_far,
+    held_near,
+    z_ref,
+    zs_ref,
     row_ref,
     slow_ref,
-    oh_ref,
-    ol_ref,
-    gh_ref,
-    gl_ref,
-    fh,
-    fl,
-    ih,
-    il,
-    tw_ref,
-    z_ref,
-    zs_ref,
     made,
     sent,
     sent_s,
@@ -221,6 +250,9 @@
     phase,
     w_high,
     w_low,
+    both_high,
+    both_low,
+    folded,
     x0,
     d0,
     x1,
@@ -233,7 +265,13 @@
     msem,
     pair_s,
     pair_r,
+    load_sem,
 ):
+    bins_ref, ops_ref, oh_ref, ol_ref, gh_ref, gl_ref, fh, fl, ih, il, tw_ref = held_near
+    loads = [
+        pltpu.make_async_copy(far, near, load_sem.at[i])
+        for i, (far, near) in enumerate(zip(held_far, held_near))
+    ]
     j, o = place_here()
     core, group = lax.rem(o, 2), o // 2
     partner = o + 1 - 2 * core
@@ -247,14 +285,32 @@
         )
         return 0
 
+    for load in loads[:2]:
+        load.start()
     lax.fori_loop(1, total, signal, 0)
-
+    for load in loads[2:]:
+        load.start()
+
+    for load in loads[:2]:
+        load.wait()
     for c in range(2):
-        source = bins_ref[c].reshape(2 * NF, BLK)
+        source = bins_ref[0, :, :, c * BLK : (c + 1) * BLK].reshape(2 * NF, BLK)
         for e in range(0, ENT, 2):
-            out = dot(source, jnp.concatenate([ops_ref[e], ops_ref[e + 1]], axis=1))
+            out = dot(source, jnp.concatenate([ops_ref[0, e], ops_ref[0, e + 1]], axis=1))
             made[c, pl.ds(e * 128, 128), :] = out[:, :BLK]
             made[c, pl.ds(e * 128 + 128, 128), :] = out[:, BLK:]
+
+    lane = lax.broadcasted_iota(jnp.int32, (ENT, NB * ENT), 1)
+    spread = (lax.rem(lane, ENT) == lax.broadcasted_iota(jnp.int32, lane.shape, 0)).astype(F32)
+    found = dot(
+        jnp.broadcast_to((targets_ref[...] + 1).astype(F32), (8, ENT)).astype(BF16),
+        spread.astype(BF16),
+    )[:1]
+    slot = lax.broadcasted_iota(jnp.int32, (1, NB * ENT), 1)
+    live = (slot // ENT == o) & (lax.rem(slot, ENT) < counts_ref[0])
+    row_ref[...] = jnp.where(live, found, 0.0)
+    for c in range(2):
+        slow_ref[c] = slow_tile(layers_ref, slowness_ref, 0, c)
 
     pl.semaphore_wait(barrier, total - 1)
 
@@ -279,21 +335,26 @@
 
     lax.fori_loop(1, MID, send_slow, 0)
 
-    def peer_at(i):
-        at = lax.rem(i * 45, total)
-        return lax.rem(j + at // OFF, MID), lax.rem(o + lax.rem(at, OFF), OFF)
-
-    def encode(i):
-        peer_j, peer_o = peer_at(i)
+    x_at, y_at, z_at = j // 2, 2 * lax.rem(j, 2) + lax.rem(o // 2, 2), o // 4
+
+    def peer_at(classes, i):
+        there, rest = [], i // 2
+        for at, distance in zip((x_at, y_at, z_at), classes):
+            step = 1 + 2 * lax.rem(rest, 2) if distance == 1 else distance
+            rest = rest // 2 if distance == 1 else rest
+            there.append(lax.rem(at + step, 4))
+        x, y, z = there
+        return 2 * x + y // 2, 4 * z + 2 * lax.rem(y, 2) + lax.rem(core + i, 2)
+
+    def encode(peer_j, peer_o):
         f, c = 8 * (peer_o // 2) + peer_j, lax.rem(peer_o, 2)
-        values = [made[c, pl.ds(part * NF + f, ENT, stride=2 * NF), :] for part in range(2)]
+        values = [made[c, pl.ds(2 * f + part, ENT, stride=2 * NF), :] for part in range(2)]
         peak = peak_of(values)
         for part in range(2):
             sent[peer_j, peer_o, part] = code(values[part], peak)
         sent_s[peer_j, peer_o] = peak * (1.0 / LEVELS)
 
-    def send(i):
-        peer_j, peer_o = peer_at(i)
+    def send(peer_j, peer_o):
         for source, target, at in ((sent, held, 0), (sent_s, held_s, 1)):
             pltpu.make_async_remote_copy(
                 source.at[peer_j, peer_o],
@@ -304,18 +365,25 @@
                 device_id_type=MESH,
             ).start()
 
-    encode(0)
-    encode(1)
-
-    def go(i, _):
-        encode(i)
-        send(i - 1)
-        return 0
-
-    lax.fori_loop(2, total, go, 0)
-    send(total - 1)
+    for classes in sorted(itertools.product(range(3), repeat=3), key=lambda d: -sum(d)):
+        first = 0 if any(classes) else 1
+        members = 2 ** (1 + classes.count(1))
+
+        def encode_one(i, _, classes=classes):
+            encode(*peer_at(classes, i))
+            return 0
+
+        def send_one(i, _, classes=classes):
+            send(*peer_at(classes, i))
+            return 0
+
+        lax.fori_loop(0, members, encode_one, 0)
+        lax.fori_loop(first, members, send_one, 0)
     pltpu.make_async_copy(sent.at[j, o], held.at[j, o], rsem.at[0]).start()
     pltpu.make_async_copy(sent_s.at[j, o], held_s.at[j, o], rsem.at[1]).start()
+
+    for load in loads[2:]:
+        load.wait()
 
     own_f = lax.broadcasted_iota(jnp.int32, (8, 128), 0) * 0 + (group * MID + j)
     omega = frequency(own_f)
@@ -326,7 +394,7 @@
         turns[jm, 0] = jnp.cos(turn)
         turns[jm, 1] = jnp.sin(turn)
     wait_bytes(rows, msem.at[0])
-    target = jnp.sum(rows[:, 0, :], axis=0, keepdims=True) - 1
+    target = jnp.sum(rows[:, 0, :], axis=0, keepdims=True).astype(jnp.int32) - 1
     spot = lax.broadcasted_iota(jnp.int32, (128, NB * ENT), 0)
     first, second = (spot == target).astype(F32), (spot + 128 == target).astype(F32)
     for p in range(2):
@@ -358,6 +426,10 @@
                 ref[core, p, part, 2 * pair + q] = out[
                     part * 128 : (part + 1) * 128, q * 128 : (q + 1) * 128
                 ]
+
+    def slots_to_waves(x_high, x_low, p):
+        high, low = w_high[p], w_low[p]
+        return dot(high, x_high) + (dot(high, x_low) + dot(low, x_high))
 
     def to_waves(pair, _):
         both = jnp.concatenate(
@@ -375,12 +447,18 @@
             ],
             axis=0,
         )
-        for p in range(2):
-            put_waves(x0, pair, p, dot_table_left(w_high[p], w_low[p], both))
+        x_high, x_low = split(both)
+        both_high[pair], both_low[pair] = x_high, x_low
+        put_waves(x0, pair, 1 - core, slots_to_waves(x_high, x_low, 1 - core))
         pair_copy(x0, pair, 0).start()
         return 0
 
+    def to_own_waves(pair, _):
+        put_waves(x0, pair, core, slots_to_waves(both_high[pair], both_low[pair], core))
+        return 0
+
     lax.fori_loop(0, MID // 2, to_waves, 0)
+    lax.fori_loop(0, MID // 2, to_own_waves, 0)
     for pair in range(MID // 2):
         pair_copy(x0, pair, 0).wait_recv()
 
@@ -411,6 +489,8 @@
     lax.fori_loop(0, 4, first_chunk, 0)
     for i in range(4):
         chunk_copy(i).wait_recv()
+
+    own_sign = (1 - 2 * core).astype(F32)
 
     def space(pair, _):
         fields = []
@@ -439,19 +519,26 @@
                     out_i.append(real * s + imag * c)
                 turned.append(jnp.concatenate(out_r + out_i, axis=0))
             ends[end] = jnp.concatenate(turned, axis=1)
-        folded = (ends[0] + ends[1], ends[0] - ends[1])
-        for p in range(2):
-            put_waves(x1, pair, p, dot_table_left(oh_ref[p], ol_ref[p], folded[p]))
+        folded[pair] = ends[0] + own_sign * ends[1]
+        other = dot_table_left(
+            oh_ref[1 - core], ol_ref[1 - core], ends[0] - own_sign * ends[1]
+        )
+        put_waves(x1, pair, 1 - core, other)
         pair_copy(x1, pair, 2).start()
         return 0
 
+    def own_space(pair, _):
+        put_waves(x1, pair, core, dot_table_left(oh_ref[core], ol_ref[core], folded[pair]))
+        return 0
+
     lax.fori_loop(0, MID // 2, space, 0)
+    lax.fori_loop(0, MID // 2, own_space, 0)
     for pair in range(MID // 2):
         pair_copy(x1, pair, 2).wait_recv()
 
     owner, mine = j // 4, lax.rem(j, 4)
     stays = owner == core
-    x_at, y_at = j // 2, lax.rem(j, 2)
+    half_at = lax.rem(j, 2)
 
     def deliver(peer, i, near):
         for source, target, at in ((coded, z_ref, 2), (coded_s, zs_ref, 3)):
@@ -489,8 +576,8 @@
             return 0
 
         lax.fori_loop(0, MID, encode_peer, 0)
-        for dx, dy in ((1, 0), (0, 1), (3, 0), (2, 1), (1, 1), (2, 0), (3, 1)):
-            peer = 2 * lax.rem(x_at + dx, 4) + lax.rem(y_at + dy, 2)
+        for dx, dy in ((2, 1), (1, 1), (3, 1), (0, 1), (2, 0), (1, 0), (3, 0)):
+            peer = 2 * lax.rem(x_at + dx, 4) + lax.rem(half_at + dy, 2)
             deliver(peer, i, False)
 
         @pl.when(stays)
@@ -533,20 +620,26 @@
             jax.ShapeDtypeStruct((4, 2, 4, 2, 2, 32, 128), jnp.int16),
             jax.ShapeDtypeStruct((4, 2, 4, 2, 1, 128), F32),
         ],
-        in_specs=[VM] * len(args),
-        out_specs=[VM] * 2,
-        scratch_shapes=[
+        in_specs=[VM] + [SM] * 3 + [ANY] * (len(args) - 4),
+        out_specs=[ANY] * 2,
+        scratch_shapes=[pltpu.VMEM(a.shape, a.dtype) for a in args[4:]]
+        + [
+            pltpu.VMEM((1, NB * ENT), F32),
+            pltpu.VMEM((2, 8, 128), F32),
             pltpu.VMEM((2, ENT * 2 * NF, BLK), F32),
             pltpu.VMEM((MID, OFF, 2, ENT, BLK), jnp.int16),
             pltpu.VMEM((MID, OFF, 1, BLK), F32),
             pltpu.VMEM((MID, NB, 2, ENT, BLK), jnp.int16),
             pltpu.VMEM((MID, NB, 1, BLK), F32),
-            pltpu.VMEM((NB, 8, NB * ENT), jnp.int32),
+            pltpu.VMEM((NB, 1, NB * ENT), F32),
             pltpu.VMEM((MID, 2, 8, 128), F32),
             pltpu.VMEM((MID, 2, 8, 128), F32),
             pltpu.VMEM((2, 16, 128, 128), F32),
             pltpu.VMEM((2, 256, 512), BF16),
             pltpu.VMEM((2, 256, 512), BF16),
+            pltpu.VMEM((4, 512, 256), BF16),
+            pltpu.VMEM((4, 512, 256), BF16),
+            pltpu.VMEM((4, 256, 256), F32),
             pltpu.VMEM(HALVES, F32),
             pltpu.VMEM(HALVES, F32),
             pltpu.VMEM(HALVES, F32),
@@ -559,6 +652,7 @@
             pltpu.SemaphoreType.DMA((4,)),
             pltpu.SemaphoreType.DMA((3, 4)),
             pltpu.SemaphoreType.DMA((3, 4)),
+            pltpu.SemaphoreType.DMA((11,)),
         ],
         compiler_params=pltpu.CompilerParams(
             collective_id=0, has_side_effects=True, vmem_limit_bytes=56 << 20
@@ -567,7 +661,7 @@
     )(*args)
 
 
-def last_kernel(z_ref, zs_ref, slow_ref, omega_ref, gh_ref, gl_ref, out_ref):
+def last_kernel(z_ref, zs_ref, layers_ref, slowness_ref, gh_ref, gl_ref, out_ref):
     fields = []
     for p in range(2):
         both = jnp.concatenate(
@@ -583,9 +677,10 @@
         )
         fields.append(dot_table_left(gh_ref[p], gl_ref[p], both))
     ends = [fields[0] + fields[1], fields[0] - fields[1]]
-    omega = omega_ref[0]
+    f = lax.axis_index("off") * 4 + pl.program_id(0)
+    omega = frequency(lax.broadcasted_iota(jnp.int32, (8, 128), 0) * 0 + f)
     for c in range(2):
-        turn = 2.0 * DZ * omega * (slow_ref[c] - 1.0)
+        turn = 2.0 * DZ * omega * (slow_tile(layers_ref, slowness_ref, 1, c) - 1.0)
         cos, sin = jnp.cos(turn), jnp.sin(turn)
         lanes = slice(c * 128, (c + 1) * 128)
         for h in range(8):
@@ -597,7 +692,7 @@
             out_ref[0, rows, 1, lanes] = real * si + imag * co
 
 
-def last(z, zs, slow, omega, inv):
+def last(z, zs, layers, slowness, inv):
     whole = pl.BlockSpec((2, 256, 256), lambda i: (0, 0, 0))
     return pl.pallas_call(
         last_kernel,
@@ -606,36 +701,34 @@
         in_specs=[
             pl.BlockSpec((1, 2, 4, 2, 2, 32, 128), lambda i: (i, 0, 0, 0, 0, 0, 0)),
             pl.BlockSpec((1, 2, 4, 2, 1, 128), lambda i: (i, 0, 0, 0, 0, 0)),
-            pl.BlockSpec((2, 8, 128), lambda i: (0, 0, 0)),
-            pl.BlockSpec((1, 8, 128), lambda i: (i, 0, 0)),
+            SM,
+            SM,
             whole,
             whole,
         ],
         out_specs=pl.BlockSpec((1, NH, 2, 256), lambda i: (i, 0, 0, 0)),
-        compiler_params=pltpu.CompilerParams(vmem_limit_bytes=40 << 20),
+        compiler_params=pltpu.CompilerParams(vmem_limit_bytes=56 << 20),
         name="last_offsets",
-    )(z, zs, slow, omega, *inv)
+    )(z, zs, layers, slowness, *inv)
 
 
 def local(bins_data, operators, targets, counts, layer_index, slowness):
-    j, o = place_here()
     (forward, inverse), (mid_fwd, mid_inv, twiddle) = offset_tables(), midpoint_tables()
-    bins = bins_data[0].reshape(NF, 2, 2, BLK).transpose(2, 1, 0, 3)
-
-    slot = lax.broadcasted_iota(jnp.int32, (8, NB * ENT), 1)
-    spread = jnp.tile(targets, (8, NB))
-    live = (slot // ENT == o) & (lax.rem(slot, ENT) < counts[0])
-    row = jnp.where(live, spread + 1, 0)
-
-    picks = layer_index[:, :, :, None] == lax.broadcasted_iota(jnp.int32, (1, 1, 1, 16), 3)
-    slow = jnp.sum(jnp.where(picks, slowness[:, None, None, :], 0.0), axis=3)
-    slow = jnp.broadcast_to(slow.transpose(0, 2, 1)[..., None], (2, 2, 8, 128))
-
+    layers = layer_index.transpose(0, 2, 1)
     z, zs = propagate(
-        bins, operators[0], row, slow[0], *forward, *inverse, *mid_fwd, *mid_inv, twiddle
+        targets,
+        counts,
+        layers,
+        slowness,
+        bins_data,
+        operators,
+        *forward,
+        *inverse,
+        *mid_fwd,
+        *mid_inv,
+        twiddle,
     )
-    own = frequency(o * 4 + lax.broadcasted_iota(jnp.int32, (4, 8, 128), 0))
-    return last(z, zs, slow[1], own, inverse)
+    return last(z, zs, layers, slowness, inverse)
 
 
 def solution(mesh):

time: 72.2 us -> 64.8 us (0.90)
  local copies, waits for them, and re-layouts: 4.4 us -> 0 us
  other arithmetic: 2.14 us -> 0 us
    pallas_call x1, Pallas kernels: 60.9 us -> 58.7 us  [propagate(): pl.pallas_call(field_kernel, out_shape=[jax.ShapeDtypeStruct((4, 2, 4, 2,...]
    unnamed x8 -> x0, local copies, waits for them, and re-layouts: 1.98 us -> none
    pallas_call x1, Pallas kernels: 3.7 us -> 5.3 us  [last(): pl.pallas_call(last_kernel, grid=(4,), out_shape=jax.ShapeDtypeStruct((4,...]
    another operation x3 -> x0, local copies, waits for them, and re-layouts: 1.53 us -> none  [the longest x2 1.53 us: local(): bins = bins_data[0].reshape(NF, 2, 2, BLK).transpose(2, 1, 0, 3)]
    reduce_sum x1 -> x0, other arithmetic: 0.85 us -> none  [local(): slow = jnp.sum(jnp.where(picks, slowness[:, None, None, :], 0.0), axis=3)]
    broadcast_in_dim x3 -> x0, local copies, waits for them, and re-layouts: 0.74 us -> none  [local(): slow = jnp.broadcast_to(slow.transpose(0, 2, 1)[..., None], (2, 2, 8, 128))]
where the time goes in v3:
time: 64.8 us; the launch traced here: 64.6 us
  Pallas kernels  64 us (99%)
  between operations  0.66 us (1%)
    pallas_call x1, Pallas kernels, propagate(): pl.pallas_call(field_kernel, out_shape=[jax.ShapeDtypeStruct((4, 2, 4, 2,...  58.7 us
    pallas_call x1, Pallas kernels, last(): pl.pallas_call(last_kernel, grid=(4,), out_shape=jax.ShapeDtypeStruct((4,...  5.3 us

profile of v3, /device:TPU:1, one launch (start us, length us, event | category | flops | bytes accessed | tf_op | source)
XLA Modules:
  0.0 64.6 jit_solution(8516690852996936269)
XLA Ops:
  0.7 58.7 %propagate.1 = (s16[4,2,4,2,2,32,128]{6,5,4,3,2,1,0:T(8,128)(2,1)}, f32[4,2,4,2,1,128]{5,4,3,2,1,0:T(1,128)}) custom-call(s32[1,16]{1,0:T(1,128)} %targets_ref.1, s32[1]{0:T(128)S(6)} %copy.16.counts_ref, s32[2,2,8]{2,1,0:T(2,128)} %bitcast.1, f32[2,16]{1,0:T(2,128)} %slowness_ref.3, bf16[1,64,2,256]{3,2,1,0:T(2,128)(2,1)} %bins_hbm.1, ...), custom_call_target="tpu_custom_call" | custom-call | tf_op jit(solution)/shard_map/propagate/pallas_call | solution.py:617
  59.3 5.3 %last_offsets.1 = f32[4,256,2,256]{3,2,1,0:T(2,128)} custom-call(s16[4,2,4,2,2,32,128]{6,5,4,3,2,1,0:T(8,128)(2,1)} %get-tuple-element.7.z_ref, f32[4,2,4,2,1,128]{5,4,3,2,1,0:T(1,128)} %get-tuple-element.8.zs_ref, s32[2,2,8]{2,1,0:T(2,128)} %bitcast.2, f32[2,16]{1,0:T(2,128)} %slowness_ref.3, bf16[2,256,256]{2,1,0:T(8,128)(2,1)} %constant.20.clone.rest_2_.gh_ref, ...), custom_call_target="tpu_custom_call" | custom-call | tf_op jit(solution)/shard_map/last_offsets/pallas_call | solution.py:697

commit v4 on v3

--- a/solution.py
+++ b/solution.py
@@ -214,7 +214,7 @@
     ops_hbm,
     *rest,
 ):
-    tables_hbm, (z_ref, zs_ref), scratch = rest[:9], rest[9:11], rest[11:]
+    tables_hbm, (z_ref, zs_ref, turn_ref), scratch = rest[:9], rest[9:12], rest[12:]
     field_body(
         targets_ref,
         counts_ref,
@@ -224,6 +224,7 @@
         scratch[:11],
         z_ref,
         zs_ref,
+        turn_ref,
         *scratch[11:],
     )
 
@@ -237,6 +238,7 @@
     held_near,
     z_ref,
     zs_ref,
+    turn_ref,
     row_ref,
     slow_ref,
     made,
@@ -266,6 +268,7 @@
     pair_s,
     pair_r,
     load_sem,
+    last_turns,
 ):
     bins_ref, ops_ref, oh_ref, ol_ref, gh_ref, gl_ref, fh, fl, ih, il, tw_ref = held_near
     loads = [
@@ -388,6 +391,15 @@
     own_f = lax.broadcasted_iota(jnp.int32, (8, 128), 0) * 0 + (group * MID + j)
     omega = frequency(own_f)
     fill_phase(phase, jnp.concatenate([omega, omega], axis=1), core)
+    for c in range(2):
+        slow = slow_tile(layers_ref, slowness_ref, 1, c)
+        for f in range(4):
+            last_f = lax.broadcasted_iota(jnp.int32, (8, 128), 0) * 0 + (o * 4 + f)
+            turn = 2.0 * DZ * frequency(last_f) * (slow - 1.0)
+            last_turns[f, c, 0] = jnp.cos(turn)
+            last_turns[f, c, 1] = jnp.sin(turn)
+    give_turns = pltpu.make_async_copy(last_turns, turn_ref, load_sem.at[11])
+    give_turns.start()
     wait_bytes(slows, msem.at[1])
     for jm in range(MID):
         turn = 2.0 * DZ * omega * (slows[jm, core] - 1.0)
@@ -531,8 +543,8 @@
         put_waves(x1, pair, core, dot_table_left(oh_ref[core], ol_ref[core], folded[pair]))
         return 0
 
-    lax.fori_loop(0, MID // 2, space, 0)
-    lax.fori_loop(0, MID // 2, own_space, 0)
+    lax.fori_loop(0, MID // 2, space, 0, unroll=2)
+    lax.fori_loop(0, MID // 2, own_space, 0, unroll=2)
     for pair in range(MID // 2):
         pair_copy(x1, pair, 2).wait_recv()
 
@@ -592,6 +604,7 @@
 
     lax.fori_loop(0, 4, second_chunk, 0)
 
+    give_turns.wait()
     for at, ref in ((0, sent), (1, sent_s)):
         wait_bytes(ref.at[0, pl.ds(0, OFF - 1)], ssem.at[at])
         wait_bytes(ref.at[pl.ds(1, MID - 1)], ssem.at[at])
@@ -619,9 +632,10 @@
         out_shape=[
             jax.ShapeDtypeStruct((4, 2, 4, 2, 2, 32, 128), jnp.int16),
             jax.ShapeDtypeStruct((4, 2, 4, 2, 1, 128), F32),
+            jax.ShapeDtypeStruct((4, 2, 2, 8, 128), F32),
         ],
         in_specs=[VM] + [SM] * 3 + [ANY] * (len(args) - 4),
-        out_specs=[ANY] * 2,
+        out_specs=[ANY] * 3,
         scratch_shapes=[pltpu.VMEM(a.shape, a.dtype) for a in args[4:]]
         + [
             pltpu.VMEM((1, NB * ENT), F32),
@@ -652,7 +666,8 @@
             pltpu.SemaphoreType.DMA((4,)),
             pltpu.SemaphoreType.DMA((3, 4)),
             pltpu.SemaphoreType.DMA((3, 4)),
-            pltpu.SemaphoreType.DMA((11,)),
+            pltpu.SemaphoreType.DMA((12,)),
+            pltpu.VMEM((4, 2, 2, 8, 128), F32),
         ],
         compiler_params=pltpu.CompilerParams(
             collective_id=0, has_side_effects=True, vmem_limit_bytes=56 << 20
@@ -661,7 +676,7 @@
     )(*args)
 
 
-def last_kernel(z_ref, zs_ref, layers_ref, slowness_ref, gh_ref, gl_ref, out_ref):
+def last_kernel(z_ref, zs_ref, turn_ref, gh_ref, gl_ref, out_ref):
     fields = []
     for p in range(2):
         both = jnp.concatenate(
@@ -677,45 +692,40 @@
         )
         fields.append(dot_table_left(gh_ref[p], gl_ref[p], both))
     ends = [fields[0] + fields[1], fields[0] - fields[1]]
-    f = lax.axis_index("off") * 4 + pl.program_id(0)
-    omega = frequency(lax.broadcasted_iota(jnp.int32, (8, 128), 0) * 0 + f)
     for c in range(2):
-        turn = 2.0 * DZ * omega * (slow_tile(layers_ref, slowness_ref, 1, c) - 1.0)
-        cos, sin = jnp.cos(turn), jnp.sin(turn)
+        cos, sin = turn_ref[0, c, 0], turn_ref[0, c, 1]
         lanes = slice(c * 128, (c + 1) * 128)
         for h in range(8):
             end, at = ends[h // 4], (h % 4) * 32
-            rows = slice(h * 32, (h + 1) * 32)
             real, imag = end[at : at + 32, lanes], end[128 + at : 160 + at, lanes]
             co, si = cos[h : h + 1], sin[h : h + 1]
-            out_ref[0, rows, 0, lanes] = real * co - imag * si
-            out_ref[0, rows, 1, lanes] = real * si + imag * co
-
-
-def last(z, zs, layers, slowness, inv):
+            for part, value in enumerate((real * co - imag * si, real * si + imag * co)):
+                out_ref[0, pl.ds(128 * h + 2 * c + part, 32, stride=4), :] = value
+
+
+def last(z, zs, turns, inv):
     whole = pl.BlockSpec((2, 256, 256), lambda i: (0, 0, 0))
     return pl.pallas_call(
         last_kernel,
         grid=(4,),
-        out_shape=jax.ShapeDtypeStruct((4, NH, 2, 256), F32),
+        out_shape=jax.ShapeDtypeStruct((4, NH * 4, 128), F32),
         in_specs=[
             pl.BlockSpec((1, 2, 4, 2, 2, 32, 128), lambda i: (i, 0, 0, 0, 0, 0, 0)),
             pl.BlockSpec((1, 2, 4, 2, 1, 128), lambda i: (i, 0, 0, 0, 0, 0)),
-            SM,
-            SM,
+            pl.BlockSpec((1, 2, 2, 8, 128), lambda i: (i, 0, 0, 0, 0)),
             whole,
             whole,
         ],
-        out_specs=pl.BlockSpec((1, NH, 2, 256), lambda i: (i, 0, 0, 0)),
+        out_specs=pl.BlockSpec((1, NH * 4, 128), lambda i: (i, 0, 0)),
         compiler_params=pltpu.CompilerParams(vmem_limit_bytes=56 << 20),
         name="last_offsets",
-    )(z, zs, layers, slowness, *inv)
+    )(z, zs, turns, *inv)
 
 
 def local(bins_data, operators, targets, counts, layer_index, slowness):
     (forward, inverse), (mid_fwd, mid_inv, twiddle) = offset_tables(), midpoint_tables()
     layers = layer_index.transpose(0, 2, 1)
-    z, zs = propagate(
+    z, zs, turns = propagate(
         targets,
         counts,
         layers,
@@ -728,7 +738,8 @@
         *mid_inv,
         twiddle,
     )
-    return last(z, zs, layers, slowness, inverse)
+    rows = last(z, zs, turns, inverse)
+    return rows.reshape(4, NH, 2, 2, 128).transpose(0, 1, 3, 2, 4).reshape(4, NH, 2, 256)
 
 
 def solution(mesh):

time: 64.8 us -> 63.8 us (0.985)
  Pallas kernels: 64 us -> 62.9 us
    pallas_call x1, Pallas kernels: 5.3 us -> 4.61 us  [last(): pl.pallas_call(last_kernel, grid=(4,), out_shape=jax.ShapeDtypeStruct((4,...]
where the time goes in v4:
time: 63.8 us; the launch traced here: 63.6 us
  Pallas kernels  62.9 us (99%)
  between operations  0.66 us (1%)
    pallas_call x1, Pallas kernels, propagate(): pl.pallas_call(field_kernel, out_shape=[jax.ShapeDtypeStruct((4, 2, 4, 2,...  58.3 us
    pallas_call x1, Pallas kernels, last(): pl.pallas_call(last_kernel, grid=(4,), out_shape=jax.ShapeDtypeStruct((4,...  4.61 us

profile of v4, /device:TPU:1, one launch (start us, length us, event | category | flops | bytes accessed | tf_op | source)
XLA Modules:
  0.0 63.6 jit_solution(44542497501934712)
XLA Ops:
  0.7 58.3 %propagate.1 = (s16[4,2,4,2,2,32,128]{6,5,4,3,2,1,0:T(8,128)(2,1)}, f32[4,2,4,2,1,128]{5,4,3,2,1,0:T(1,128)}, f32[4,2,2,8,128]{4,3,2,1,0:T(8,128)}) custom-call(s32[1,16]{1,0:T(1,128)} %targets_ref.1, s32[1]{0:T(128)S(6)} %copy.17.counts_ref, s32[2,2,8]{2,1,0:T(2,128)} %bitcast.6, f32[2,16]{1,0:T(2,128)} %slowness_ref.1, bf16[1,64,2,256]{3,2,1,0:T(2,128)(2,1)} %bins_hbm.1, ...), custom_call_target="tpu_custom_call" | custom-call | tf_op jit(solution)/shard_map/propagate/pallas_call | solution.py:630
  58.9 4.6 %last_offsets.1 = f32[4,1024,128]{2,1,0:T(8,128)} custom-call(s16[4,2,4,2,2,32,128]{6,5,4,3,2,1,0:T(8,128)(2,1)} %get-tuple-element.8.z_ref, f32[4,2,4,2,1,128]{5,4,3,2,1,0:T(1,128)} %get-tuple-element.9.zs_ref, f32[4,2,2,8,128]{4,3,2,1,0:T(8,128)} %get-tuple-element.10.turn_ref, bf16[2,256,256]{2,1,0:T(8,128)(2,1)} %constant.20.clone.rest_2_.gh_ref, ...), custom_call_target="tpu_custom_call" | custom-call | tf_op jit(solution)/shard_map/last_offsets/pallas_call | solution.py:708

commit v5 on v4

--- a/solution.py
+++ b/solution.py
@@ -380,7 +380,7 @@
             send(*peer_at(classes, i))
             return 0
 
-        lax.fori_loop(0, members, encode_one, 0)
+        lax.fori_loop(0, members, encode_one, 0, unroll=2)
         lax.fori_loop(first, members, send_one, 0)
     pltpu.make_async_copy(sent.at[j, o], held.at[j, o], rsem.at[0]).start()
     pltpu.make_async_copy(sent_s.at[j, o], held_s.at[j, o], rsem.at[1]).start()

time: 63.8 us -> 63.7 us (level)
  no operation moved by 1% of the time
where the time goes in v5:
time: 63.7 us; the launch traced here: 63.5 us
  Pallas kernels  62.9 us (99%)
  between operations  0.66 us (1%)
    pallas_call x1, Pallas kernels, propagate(): pl.pallas_call(field_kernel, out_shape=[jax.ShapeDtypeStruct((4, 2, 4, 2,...  58.3 us
    pallas_call x1, Pallas kernels, last(): pl.pallas_call(last_kernel, grid=(4,), out_shape=jax.ShapeDtypeStruct((4,...  4.61 us

profile of v5, /device:TPU:1, one launch (start us, length us, event | category | flops | bytes accessed | tf_op | source)
XLA Modules:
  0.0 63.5 jit_solution(11632949189118735721)
XLA Ops:
  0.7 58.3 %propagate.1 = (s16[4,2,4,2,2,32,128]{6,5,4,3,2,1,0:T(8,128)(2,1)}, f32[4,2,4,2,1,128]{5,4,3,2,1,0:T(1,128)}, f32[4,2,2,8,128]{4,3,2,1,0:T(8,128)}) custom-call(s32[1,16]{1,0:T(1,128)} %targets_ref.1, s32[1]{0:T(128)S(6)} %copy.17.counts_ref, s32[2,2,8]{2,1,0:T(2,128)} %bitcast.6, f32[2,16]{1,0:T(2,128)} %slowness_ref.1, bf16[1,64,2,256]{3,2,1,0:T(2,128)(2,1)} %bins_hbm.1, ...), custom_call_target="tpu_custom_call" | custom-call | tf_op jit(solution)/shard_map/propagate/pallas_call | solution.py:630
  58.9 4.6 %last_offsets.1 = f32[4,1024,128]{2,1,0:T(8,128)} custom-call(s16[4,2,4,2,2,32,128]{6,5,4,3,2,1,0:T(8,128)(2,1)} %get-tuple-element.8.z_ref, f32[4,2,4,2,1,128]{5,4,3,2,1,0:T(1,128)} %get-tuple-element.9.zs_ref, f32[4,2,2,8,128]{4,3,2,1,0:T(8,128)} %get-tuple-element.10.turn_ref, bf16[2,256,256]{2,1,0:T(8,128)(2,1)} %constant.20.clone.rest_2_.gh_ref, ...), custom_call_target="tpu_custom_call" | custom-call | tf_op jit(solution)/shard_map/last_offsets/pallas_call | solution.py:708
